TPU v7x, 32 devices: a whole 2x2x4 slice. The times are simulated.
32 devices in a mesh: beam: 2 (over x), freq: 8 (over z, y), tm: 2 (over core).
Axes of the slice: x: 2, y: 2, z: 4, core: 2. Of those that a mesh axis runs over, the one named last changes fastest.
Arguments:
- spectra: float32 [4096, 5120], P(('beam', 'freq'), 'tm'), parts along dimension 0, may hold values from -6 to 6
- delays: int32 [11, 2048], replicated, may hold values from 0 to 1024, as said below
- widths: int32 [8], replicated, may hold values from 1 to 128, as said below
Outputs:
- filtered: float32 [8, 4096, 5120], P(None, ('beam', 'freq'), 'tm'), parts along dimension 1
There are 2 independent parts, one for each index of `beam`. A program takes and returns all parts, laid end to end along the dimension named above; an argument that names none is the same for every part. Nothing has to cross between parts.
Inputs may be any that keep to these rules, and one draw needn't show every extreme that they name: delays[l, r] lies in 0 to 2 ** l, and every level l has some entry equal to 2 ** l. The widths include 1 and 128.
All inputs are finite; a program needn't handle non-finite values.
Results may differ from a plain program's by a relative error of at most 0.0003.
Values sent between devices are 32-bit elements; how exact they have to be, the bound alone decides.
A program may use at most 192 MiB of HBM per device.

v0:
```python
import functools

import jax
import jax.numpy as jnp
from jax import lax
from jax.experimental import pallas as pl
from jax.experimental.pallas import tpu as pltpu
from jax.sharding import PartitionSpec as P

LANES = 128
SUB = 8
TAPS = 128
VMEM = pltpu.MemorySpace.VMEM
SMEM = pltpu.MemorySpace.SMEM


def cdiv(a, b):
    return -(-a // b)


def round_up(a, b):
    return cdiv(a, b) * b


def shifted(src, start, width, shift, reach, lane):
    if reach >= LANES:
        start = start + lax.shift_right_logical(shift, LANES.bit_length() - 1)
        shift = shift & (LANES - 1)
    low = src[pl.ds(start, width), :]
    high = src[pl.ds(start + 1, width), :]
    return pltpu.roll(jnp.where(lane < shift, high, low), LANES - shift, 1)


def local_tree_kernel(levels, blocks, lead_blocks, own, pitch, spectra, lead, shifts, *refs):
    *outs, buf_a, buf_b = refs
    rows = spectra.shape[0]
    groups = len(outs)
    per = own // groups
    per_bits, own_bits = per.bit_length() - 1, own.bit_length() - 1
    lane = lax.broadcasted_iota(jnp.int32, (pitch, LANES), 1)
    out_lane = lax.broadcasted_iota(jnp.int32, (blocks, LANES), 1)

    def spread(group, carry):
        at = pl.ds(pl.multiple_of(group * SUB, SUB), SUB)
        for b in range(blocks + lead_blocks):
            if b < blocks:
                v = spectra[at, b * LANES : (b + 1) * LANES]
            else:
                v = lead[at, (b - blocks) * LANES : (b - blocks + 1) * LANES]
            buf_a[pl.ds(group * (SUB * pitch) + b, SUB, stride=pitch), :] = v
        return carry

    lax.fori_loop(0, rows // SUB, spread, 0)

    src, dst = buf_a, buf_b
    for level in range(levels - 1):
        half = 2**level
        unroll = min(8, rows // 2)

        def pairs(n, carry, src=src, dst=dst, half=half, level=level):
            for u in range(unroll):
                p = n * unroll + u
                row_a = ((p >> level) << (level + 1)) + (p & (half - 1))
                at_a = pl.multiple_of(row_a * pitch, SUB)
                at_b = pl.multiple_of((row_a + half) * pitch, SUB)
                a = src[pl.ds(at_a, pitch), :]
                for e, at in enumerate((at_a, at_b)):
                    shift = shifts[level * rows + row_a + e * half]
                    dst[pl.ds(at, pitch), :] = a + shifted(src, at_b, pitch, shift, half, lane)
            return carry

        lax.fori_loop(0, rows // 2 // unroll, pairs, 0)
        src, dst = dst, src

    level = levels - 1
    half = 2**level
    for group, out in enumerate(outs):
        unroll = 8 if rows // 2 // groups % 8 == 0 else 1

        def last_pairs(n, carry, src=src, out=out, group=group):
            for u in range(unroll):
                m = n * unroll + u
                row_a = (m >> per_bits) * own + group * per + (m & (per - 1))
                at_a = pl.multiple_of(row_a * pitch, SUB)
                at_b = pl.multiple_of((row_a + half) * pitch, SUB)
                a = src[pl.ds(at_a, blocks), :]
                for e in range(2):
                    row = row_a + e * half
                    shift = shifts[level * rows + row]
                    at = ((row >> own_bits) * per + (m & (per - 1))) * blocks
                    out[pl.ds(at, blocks), :] = a + shifted(src, at_b, blocks, shift, half, out_lane)
            return carry

        lax.fori_loop(0, rows // 2 // groups // unroll, last_pairs, 0)


def local_tree(spectra, lead, shifts, parts, groups):
    rows, span = spectra.shape
    levels = rows.bit_length() - 1
    blocks = span // LANES
    lead_blocks = lead.shape[1] // LANES
    own = rows // parts
    pitch = round_up(blocks + lead_blocks, SUB)
    spec = pl.BlockSpec(memory_space=VMEM)
    buf = pltpu.VMEM((rows * pitch + SUB, LANES), jnp.float32)
    shape = jax.ShapeDtypeStruct((rows // groups * blocks, LANES), jnp.float32)
    return pl.pallas_call(
        functools.partial(local_tree_kernel, levels, blocks, lead_blocks, own, pitch),
        out_shape=[shape] * groups,
        in_specs=[spec, spec, pl.BlockSpec(memory_space=SMEM)],
        out_specs=[spec] * groups,
        scratch_shapes=[buf, buf],
    )(spectra, lead, shifts)


def turn_kernel(bits, rows, blocks, halves, pitch, first_level, groups, shifts, *refs):
    xs, outs = refs[:groups], refs[groups : 2 * groups]
    arrived, ready = refs[2 * groups : 3 * groups], refs[3 * groups : 4 * groups]
    buf_a, buf_b, sems, own_sems = refs[4 * groups :]
    own = rows * groups
    total = blocks * halves
    bands = 2**bits
    parts = bands * halves
    out_blocks = blocks + 1
    me = lax.axis_index("freq") * halves + lax.axis_index("tm")
    beam = lax.axis_index("beam")

    def device(k):
        other = (me + k) % parts
        return other, (beam, other // halves, other % halves)

    barrier = pltpu.get_barrier_semaphore()
    for k in range(1, parts):
        pl.semaphore_signal(
            barrier, inc=1, device_id=device(k)[1], device_id_type=pl.DeviceIdType.MESH
        )
    pl.semaphore_wait(barrier, parts - 1)

    def send(src, dst, turn):
        copies = []
        for k in range(1, parts):
            other, where = device(k)
            c = pltpu.make_async_remote_copy(
                src_ref=src.at[other],
                dst_ref=dst.at[me],
                send_sem=sems.at[0, turn, k],
                recv_sem=sems.at[1, turn, k],
                device_id=where,
                device_id_type=pl.DeviceIdType.MESH,
            )
            c.start()
            copies.append(c)
        c = pltpu.make_async_copy(src.at[me], dst.at[me], own_sems.at[turn])
        c.start()
        copies.append(c)
        return copies

    def wait(copies):
        for c in copies:
            c.wait()

    first = [send(xs[g], arrived[g], g) for g in range(groups)]

    lane = lax.broadcasted_iota(jnp.int32, (total, LANES), 1)
    out_lane = lax.broadcasted_iota(jnp.int32, (out_blocks, LANES), 1)
    zero = jnp.zeros((pitch - total, LANES), jnp.float32)

    def clear(r, carry):
        for buf in (buf_a, buf_b):
            buf[pl.ds(r * pitch + total, pitch - total), :] = zero
        return carry

    lax.fori_loop(0, bands * rows, clear, 0)
    for buf in (buf_a, buf_b):
        buf[pl.ds(bands * rows * pitch, SUB), :] = jnp.zeros((SUB, LANES), jnp.float32)

    back = []
    for g in range(groups):
        wait(first[g])

        def gather(i, carry, g=g):
            for s in range(bands):
                at = (s * rows + i) * pitch
                for c in range(halves):
                    piece = arrived[g][s * halves + c, pl.ds(i * blocks, blocks), :]
                    buf_a[pl.ds(at + c * blocks, blocks), :] = piece
            return carry

        lax.fori_loop(0, rows, gather, 0)

        src, dst = buf_a, buf_b
        for level in range(bits):
            step = 2**level
            reach = 2 ** (first_level + level)

            def one_row(i, carry, src=src, dst=dst, step=step, level=level, reach=reach, g=g):
                for j in range(bands):
                    base = (j // (2 * step)) * (2 * step) + j % step
                    shift = shifts[(level * bands + j) * own + g * rows + i]
                    at_a = pl.multiple_of((base * rows + i) * pitch, SUB)
                    at_b = pl.multiple_of(((base + step) * rows + i) * pitch, SUB)
                    if level < bits - 1:
                        a = src[pl.ds(at_a, total), :]
                        at = pl.multiple_of((j * rows + i) * pitch, SUB)
                        dst[pl.ds(at, total), :] = a + shifted(src, at_b, total, shift, reach, lane)
                        continue
                    for c in range(halves):
                        a = src[pl.ds(at_a + c * blocks, out_blocks), :]
                        moved = shifted(src, at_b + c * blocks, out_blocks, shift, reach, out_lane)
                        ready[g][j * halves + c, pl.ds(i * out_blocks, out_blocks), :] = a + moved
                return carry

            lax.fori_loop(0, rows, one_row, 0)
            src, dst = dst, src
        back.append(send(ready[g], outs[g], groups + g))
    for copies in back:
        wait(copies)


def turn_and_cross(sections, shifts, bits, own, blocks, halves, first_level):
    groups = len(sections)
    bands = 2**bits
    parts = bands * halves
    reach = 2 ** (first_level + bits - 1)
    pitch = round_up(blocks * halves + cdiv(reach, LANES) + 2, SUB)
    rows = own // groups
    buf = pltpu.VMEM((bands * rows * pitch + SUB, LANES), jnp.float32)
    here = pl.BlockSpec(memory_space=pl.ANY)
    out_shape = jax.ShapeDtypeStruct((parts, rows * (blocks + 1), LANES), jnp.float32)
    return pl.pallas_call(
        functools.partial(turn_kernel, bits, rows, blocks, halves, pitch, first_level, groups),
        out_shape=[out_shape] * groups,
        in_specs=[pl.BlockSpec(memory_space=SMEM)] + [here] * groups,
        out_specs=[here] * groups,
        scratch_shapes=[pltpu.VMEM((parts, rows * blocks, LANES), jnp.float32)] * groups
        + [pltpu.VMEM((parts, rows * (blocks + 1), LANES), jnp.float32)] * groups
        + [buf, buf]
        + [
            pltpu.SemaphoreType.DMA((2, 2 * groups, parts)),
            pltpu.SemaphoreType.DMA((2 * groups,)),
        ],
        compiler_params=pltpu.CompilerParams(collective_id=0, has_side_effects=True),
    )(shifts, *sections)


def filter_kernel(per_step, blocks, filters, widths, scaling, x, *refs):
    out, matrix = refs[-2:]
    rows = out.shape[1] * out.shape[2]

    @pl.when(pl.program_id(0) == 0)
    def _():
        pos = lax.broadcasted_iota(jnp.int32, (2 * TAPS, TAPS), 0)
        dist = pos - lax.broadcasted_iota(jnp.int32, (2 * TAPS, TAPS), 1)
        for w in range(filters):
            box = (dist >= 0) & (dist < widths[w])
            value = jnp.where(box, 1.0, 0.0).astype(jnp.bfloat16)
            for n in range(2):
                matrix[n * 2 * TAPS : (n + 1) * 2 * TAPS, w * TAPS : (w + 1) * TAPS] = value

    first = pl.program_id(0) * per_step
    pieces = [x[pl.ds(first + n, rows, stride=blocks + 1), :] for n in range(per_step + 1)]
    heads = [v.astype(jnp.bfloat16) for v in pieces]
    tails = [(v - h.astype(jnp.float32)).astype(jnp.bfloat16) for v, h in zip(pieces, heads)]
    together = 2 if filters % 2 == 0 else 1
    for k in range(per_step):
        lhs = jnp.concatenate([heads[k], heads[k + 1], tails[k], tails[k + 1]], axis=1)
        for w in range(0, filters, together):
            m = matrix[:, w * TAPS : (w + together) * TAPS]
            y = jnp.dot(lhs, m, preferred_element_type=jnp.float32)
            for n in range(together):
                part = y[:, n * TAPS : (n + 1) * TAPS] * scaling[w + n]
                out[w + n, :, :, k * LANES : (k + 1) * LANES] = part.reshape(out.shape[1], out.shape[2], LANES)


def filter_rows(x, into, widths, scaling, parts, own, group, groups, blocks):
    filters = widths.shape[0]
    per_step = 4 if blocks % 4 == 0 else 1
    rows = own // groups
    if rows % SUB:
        view, block, where = (filters, 1, parts * own), (filters, 1, parts * own), (0, 0, 0)
    else:
        view, block, where = (filters, parts, own), (filters, parts, rows), (0, 0, group)
    specs = [
        pl.BlockSpec(memory_space=SMEM),
        pl.BlockSpec(memory_space=SMEM),
        pl.BlockSpec(memory_space=VMEM),
    ]
    args = [widths, scaling, x]
    if into is not None:
        specs.append(pl.BlockSpec(memory_space=pl.ANY))
        args.append(into)
    cells = filters * parts * rows * blocks * LANES
    return pl.pallas_call(
        functools.partial(filter_kernel, per_step, blocks, filters),
        grid=(blocks // per_step,),
        out_shape=jax.ShapeDtypeStruct(view + (blocks * LANES,), jnp.float32),
        in_specs=specs,
        out_specs=pl.BlockSpec(block + (per_step * LANES,), lambda s: where + (s,)),
        scratch_shapes=[pltpu.VMEM((4 * TAPS, filters * TAPS), jnp.bfloat16)],
        input_output_aliases={} if into is None else {3: 0},
        cost_estimate=pl.CostEstimate(flops=1024 * cells, bytes_accessed=4 * cells, transcendentals=0),
    )(*args)


GROUPS = 2


def local(spectra, delays, widths):
    rows, span = spectra.shape
    all_levels, all_rows = delays.shape
    levels = rows.bit_length() - 1
    bits = all_levels - levels
    bands, halves = lax.axis_size("freq"), lax.axis_size("tm")
    parts = bands * halves
    own = rows // parts
    groups = GROUPS if own % (SUB * GROUPS) == 0 else 1
    blocks = span // LANES
    lead_width = cdiv(rows - 1, LANES) * LANES
    position = lax.axis_index("freq")
    lead = lax.ppermute(spectra[:, :lead_width], "tm", [(k, k - 1) for k in range(1, halves)])
    own_shifts = lax.dynamic_slice_in_dim(delays[:levels], position * rows, rows, 1).reshape(-1)
    mine = (position * halves + lax.axis_index("tm")) * own
    shifts = lax.dynamic_slice_in_dim(delays[levels:].reshape(bits, bands, rows), mine, own, 2)
    shifts = shifts.reshape(-1)
    scaling = 1.0 / jnp.sqrt(widths.astype(jnp.float32) * all_rows)

    sections = local_tree(spectra, lead, own_shifts, parts, groups)
    sections = [x.reshape(parts, -1, LANES) for x in sections]
    rows_done = turn_and_cross(sections, shifts, bits, own, blocks, halves, levels)
    filtered = None
    for g, x in enumerate(rows_done):
        x = x.reshape(-1, LANES)
        filtered = filter_rows(x, filtered, widths, scaling, parts, own, g, groups, blocks)
    return filtered.reshape(widths.shape[0], rows, span)


def solution(mesh):
    return jax.shard_map(
        local,
        mesh=mesh,
        in_specs=(P(("beam", "freq"), "tm"), P(), P()),
        out_specs=P(None, ("beam", "freq"), "tm"),
        check_vma=False,
    )
```

profile of v0, /device:TPU:15, one launch (start us, length us, event | category | flops | bytes accessed | tf_op | source)
XLA Modules:
  0.0 167.4 jit_solution(962272217966177691)
XLA Ops:
  0.0 1.0 slice.10
  1.0 2.6 %collective-permute-start = (f32[256,256]{1,0:T(8,128)S(1)}, f32[256,256]{1,0:T(8,128)S(1)}, u32[]{:S(2)}, u32[]{:S(2)}) collective-permute-start(f32[256,256]{1,0:T(8,128)S(1)} %slice.10), channel_id=1, source_target_pairs={{1,0},{3,2},{5,4},{7,6},{9,8},{11,10},{13,12},{15,14},{17,16},{19,... | collective-permute-start | bytes 786440 | tf_op jit(solution)/shard_map/ppermute | solution.py:320
  3.6 0.8 slice.9
  4.4 0.8 slice.11
  5.3 0.1 constant_dynamic-slice_fusion
  5.4 0.7 reshape.25.shifts
  6.0 0.6 copy.6
  6.6 1.3 multiply_rsqrt_fusion.scaling
  7.9 0.0 collective-permute-done.lead
  7.9 0.0 copy-start
  7.9 0.7 copy-done
  8.6 19.4 %shard_map.37 = (f32[2560,128]{1,0:T(8,128)}, f32[2560,128]{1,0:T(8,128)}) custom-call(f32[256,2560]{1,0:T(8,128)} %spectra.1, f32[256,256]{1,0:T(8,128)} %copy-done, s32[2048]{0:T(1024)} %bitcast.18), custom_call_target="tpu_custom_call" | custom-call | tf_op jit(solution)/shard_map/pallas_call | solution.py:107
  28.0 123.5 %shard_map.38 = (f32[16,168,128]{2,1,0:T(8,128)}, f32[16,168,128]{2,1,0:T(8,128)}) custom-call(s32[384]{0:T(512)} %reshape.25.shifts, f32[16,160,128]{2,1,0:T(8,128)} %bitcast.14, f32[16,160,128]{2,1,0:T(8,128)} %bitcast.15), custom_call_target="tpu_custom_call" | custom-call | tf_op jit(solution)/shard_map/pallas_call | solution.py:230
  151.5 8.0 %shard_map.39.refs_0_ = f32[8,16,16,2560]{3,2,1,0:T(8,128)} custom-call(s32[8]{0:T(128)} %widths.3, f32[8]{0:T(128)} %multiply_rsqrt_fusion.scaling, f32[2688,128]{1,0:T(8,128)} %bitcast.13), custom_call_target="tpu_custom_call" | custom-call | flops 2684354560 | bytes 10485760 | tf_op jit(solution)/shard_map/pallas_call | solution.py:293
  159.4 7.9 %shard_map.40 = f32[8,16,16,2560]{3,2,1,0:T(8,128)} custom-call(s32[8]{0:T(128)} %widths.3, f32[8]{0:T(128)} %multiply_rsqrt_fusion.scaling, f32[2688,128]{1,0:T(8,128)} %bitcast.12, f32[8,16,16,2560]{3,2,1,0:T(8,128)} %shard_map.39.refs_0_), custom_call_target="tpu_custom_call", output_to_operand_aliasing={{}: (3, {})} | custom-call | flops 2684354560 | bytes 10485760 | tf_op jit(solution)/shard_map/pallas_call | solution.py:293
  (2 shorter events, 0.0 us)
Async XLA Ops:
  1.0 6.9 %collective-permute-start = (f32[256,256]{1,0:T(8,128)S(1)}, f32[256,256]{1,0:T(8,128)S(1)}, u32[]{:S(2)}, u32[]{:S(2)}) collective-permute-start(f32[256,256]{1,0:T(8,128)S(1)} %slice.10), channel_id=1, source_target_pairs={{1,0},{3,2},{5,4},{7,6},{9,8},{11,10},{13,12},{15,14},{17,16},{19,... | collective-permute-start | bytes 786440 | tf_op jit(solution)/shard_map/ppermute | solution.py:320
  7.9 0.7 copy-start
where the time goes:
time: 168 us; the launch traced here: 167 us
  Pallas kernels  159 us (95%)
  local copies, waits for them, and re-layouts  4.7 us (3%)
  starting transfers between devices  2.6 us (2%)
    pallas_call x1, Pallas kernels, turn_and_cross(): pl.pallas_call(functools.partial(turn_kernel, bits, rows, blocks, halves,...  123 us
    pallas_call x1, Pallas kernels, local_tree(): pl.pallas_call(functools.partial(local_tree_kernel, levels, blocks, lead_...  19.4 us
    pallas_call x2, Pallas kernels, filter_rows(): pl.pallas_call(functools.partial(filter_kernel, per_step, blocks, filters...  15.9 us
  transfers between devices with their start and end apart: 1, of which 0 were waited for; matrix products, arithmetic and copies ran while one was open for 3% of the time, Pallas kernels for 0%

commit v1 on v0

v1 whole, which is shorter than its diff:
```python
import functools

import jax
import jax.numpy as jnp
from jax import lax
from jax.experimental import pallas as pl
from jax.experimental.pallas import tpu as pltpu
from jax.sharding import PartitionSpec as P

LANES = 128
SUB = 8
TAPS = 128
VMEM = pltpu.MemorySpace.VMEM
SMEM = pltpu.MemorySpace.SMEM
MESH = pl.DeviceIdType.MESH


def cdiv(a, b):
    return -(-a // b)


def round_up(a, b):
    return cdiv(a, b) * b


def shifted(src, start, width, shift, reach, lane):
    if reach >= LANES:
        start = start + lax.shift_right_logical(shift, LANES.bit_length() - 1)
        shift = shift & (LANES - 1)
    low = src[pl.ds(start, width), :]
    high = src[pl.ds(start + 1, width), :]
    return pltpu.roll(jnp.where(lane < shift, high, low), LANES - shift, 1)


class Plan:
    def __init__(self, rows, span, all_levels, all_rows, bands, halves, groups):
        self.rows, self.span = rows, span
        self.all_levels, self.all_rows = all_levels, all_rows
        self.levels = rows.bit_length() - 1
        self.bits = all_levels - self.levels
        self.bands, self.halves = bands, halves
        self.parts = bands * halves
        self.own = rows // self.parts
        self.groups = groups if self.own % (SUB * groups) == 0 else 1
        self.per = self.own // self.groups
        self.blocks = span // LANES
        self.lead_blocks = cdiv(rows - 1, LANES)
        self.blocks_a = SUB - self.lead_blocks
        self.blocks_b = self.blocks - self.blocks_a
        self.pitch_a = SUB
        self.pitch_b = round_up(self.blocks_b + self.lead_blocks, SUB)
        self.total = self.blocks * halves
        reach = 2 ** (all_levels - 1)
        self.pitch_x = round_up(self.total + cdiv(reach, LANES) + 2, SUB)
        self.out_blocks = self.blocks + 1


def tree_kernel(plan, delays, spectra, *refs):
    p = plan
    G, parts, halves, bands = p.groups, p.parts, p.halves, p.bands
    refs = list(refs)

    def take(n):
        got = refs[:n]
        del refs[:n]
        return got

    outs = take(G)
    (rows_in, lead) = take(2)
    tree_a, tree_b = take(2), take(2)
    (send_a,) = take(1)
    send_b = take(G)
    (came_a,) = take(1)
    came_b = take(G)
    ready = take(G)
    buf_a, buf_b = take(2)
    sems, own_sems, in_sems, lead_sems = take(4)

    beam, freq, tm = (lax.axis_index(n) for n in ("beam", "freq", "tm"))
    me = freq * halves + tm
    head = SUB * LANES

    load_a = pltpu.make_async_copy(spectra.at[:, :head], rows_in.at[:, :head], in_sems.at[0])
    load_b = pltpu.make_async_copy(spectra.at[:, head:], rows_in.at[:, head:], in_sems.at[1])
    load_a.start()
    load_b.start()

    def peer(k):
        other = me
        step = 1
        while step < parts:
            if k & step:
                other = other + step * (1 - 2 * ((me // step) % 2))
            step *= 2
        return other, (beam, other // halves, other % halves)

    barrier = pltpu.get_barrier_semaphore()
    for k in range(1, parts):
        pl.semaphore_signal(barrier, inc=1, device_id=peer(k)[1], device_id_type=MESH)

    def spread(buf, pitch, first, count, lead_count):
        def body(n, carry):
            at = pl.ds(pl.multiple_of(n * SUB, SUB), SUB)
            for b in range(count):
                v = rows_in[at, (first + b) * LANES : (first + b + 1) * LANES]
                buf[pl.ds(n * (SUB * pitch) + b, SUB, stride=pitch), :] = v
            for b in range(lead_count):
                v = lead[at, b * LANES : (b + 1) * LANES]
                v = jnp.where(tm < halves - 1, v, 0.0)
                buf[pl.ds(n * (SUB * pitch) + count + b, SUB, stride=pitch), :] = v
            return carry

        lax.fori_loop(0, p.rows // SUB, body, 0)

    mine = freq * p.rows

    def levels(bufs, pitch):
        lane = lax.broadcasted_iota(jnp.int32, (pitch, LANES), 1)
        src, dst = bufs
        for level in range(p.levels - 1):
            half = 2**level
            unroll = min(8, p.rows // 2)

            def pairs(n, carry, src=src, dst=dst, half=half, level=level):
                for u in range(unroll):
                    q = n * unroll + u
                    row_a = ((q >> level) << (level + 1)) + (q & (half - 1))
                    at_a = pl.multiple_of(row_a * pitch, SUB)
                    at_b = pl.multiple_of((row_a + half) * pitch, SUB)
                    a = src[pl.ds(at_a, pitch), :]
                    for e, at in enumerate((at_a, at_b)):
                        shift = delays[level, mine + row_a + e * half]
                        dst[pl.ds(at, pitch), :] = a + shifted(src, at_b, pitch, shift, half, lane)
                return carry

            lax.fori_loop(0, p.rows // 2 // unroll, pairs, 0)
            src, dst = dst, src
        return src

    def last_level(src, pitch, out, blocks, group, per):
        level = p.levels - 1
        half = 2**level
        per_bits, own_bits = per.bit_length() - 1, p.own.bit_length() - 1
        lane = lax.broadcasted_iota(jnp.int32, (blocks, LANES), 1)
        count = p.rows // 2 * per // p.own
        unroll = 8 if count % 8 == 0 else 1

        def last_pairs(n, carry):
            for u in range(unroll):
                m = n * unroll + u
                row_a = (m >> per_bits) * p.own + group * per + (m & (per - 1))
                at_a = pl.multiple_of(row_a * pitch, SUB)
                at_b = pl.multiple_of((row_a + half) * pitch, SUB)
                a = src[pl.ds(at_a, blocks), :]
                for e in range(2):
                    row = row_a + e * half
                    shift = delays[level, mine + row]
                    at = (m & (per - 1)) * blocks
                    out[row >> own_bits, pl.ds(at, blocks), :] = a + shifted(
                        src, at_b, blocks, shift, half, lane
                    )
            return carry

        lax.fori_loop(0, count // unroll, last_pairs, 0)

    def send(src, dst, turn):
        copies = []
        for k in range(parts - 1, 0, -1):
            other, where = peer(k)
            c = pltpu.make_async_remote_copy(
                src_ref=src.at[other],
                dst_ref=dst.at[me],
                send_sem=sems.at[0, turn, k],
                recv_sem=sems.at[1, turn, k],
                device_id=where,
                device_id_type=MESH,
            )
            c.start()
            copies.append(c)
        c = pltpu.make_async_copy(src.at[me], dst.at[me], own_sems.at[turn])
        c.start()
        return copies, c

    def arrive(sent):
        for c in sent[0]:
            c.wait_recv()
        sent[1].wait()

    load_a.wait()
    spread(tree_a[0], p.pitch_a, 0, min(SUB, p.blocks), 0)
    src = levels(tree_a, p.pitch_a)
    last_level(src, p.pitch_a, send_a, p.blocks_a, 0, p.own)

    pl.semaphore_wait(barrier, parts - 1)
    left = (tm + halves - 1) % halves
    get_lead = pltpu.make_async_remote_copy(
        src_ref=spectra.at[:, : p.lead_blocks * LANES],
        dst_ref=lead,
        send_sem=lead_sems.at[0],
        recv_sem=lead_sems.at[1],
        device_id=(beam, freq, left),
        device_id_type=MESH,
    )
    get_lead.start()
    sent_a = send(send_a, came_a, 0)

    load_b.wait()
    get_lead.wait()
    spread(tree_b[0], p.pitch_b, p.blocks_a, p.blocks_b, p.lead_blocks)
    src = levels(tree_b, p.pitch_b)
    sent_b = []
    for g in range(G):
        last_level(src, p.pitch_b, send_b[g], p.blocks_b, g, p.per)
        sent_b.append(send(send_b[g], came_b[g], 1 + g))

    total, pitch, rows = p.total, p.pitch_x, p.per
    lane = lax.broadcasted_iota(jnp.int32, (total, LANES), 1)
    out_lane = lax.broadcasted_iota(jnp.int32, (p.out_blocks, LANES), 1)
    zero = jnp.zeros((pitch - total, LANES), jnp.float32)

    def clear(r, carry):
        for buf in (buf_a, buf_b):
            buf[pl.ds(r * pitch + total, pitch - total), :] = zero
        return carry

    lax.fori_loop(0, bands * rows, clear, 0)
    for buf in (buf_a, buf_b):
        buf[pl.ds(bands * rows * pitch, SUB), :] = jnp.zeros((SUB, LANES), jnp.float32)

    back = []
    arrive(sent_a)
    for g in range(G):
        arrive(sent_b[g])

        def gather(i, carry, g=g):
            for s in range(bands):
                at = (s * rows + i) * pitch
                for c in range(halves):
                    piece = came_a[s * halves + c, pl.ds((g * rows + i) * p.blocks_a, p.blocks_a), :]
                    buf_a[pl.ds(at + c * p.blocks, p.blocks_a), :] = piece
                    piece = came_b[g][s * halves + c, pl.ds(i * p.blocks_b, p.blocks_b), :]
                    buf_a[pl.ds(at + c * p.blocks + p.blocks_a, p.blocks_b), :] = piece
            return carry

        lax.fori_loop(0, rows, gather, 0)

        src, dst = buf_a, buf_b
        for level in range(p.bits):
            step = 2**level
            reach = 2 ** (p.levels + level)

            def one_row(i, carry, src=src, dst=dst, step=step, level=level, reach=reach, g=g):
                for j in range(bands):
                    base = (j // (2 * step)) * (2 * step) + j % step
                    shift = delays[p.levels + level, j * p.rows + me * p.own + g * rows + i]
                    at_a = pl.multiple_of((base * rows + i) * pitch, SUB)
                    at_b = pl.multiple_of(((base + step) * rows + i) * pitch, SUB)
                    if level < p.bits - 1:
                        a = src[pl.ds(at_a, total), :]
                        at = pl.multiple_of((j * rows + i) * pitch, SUB)
                        dst[pl.ds(at, total), :] = a + shifted(src, at_b, total, shift, reach, lane)
                        continue
                    for c in range(halves):
                        a = src[pl.ds(at_a + c * p.blocks, p.out_blocks), :]
                        moved = shifted(src, at_b + c * p.blocks, p.out_blocks, shift, reach, out_lane)
                        ready[g][j * halves + c, pl.ds(i * p.out_blocks, p.out_blocks), :] = a + moved
                return carry

            lax.fori_loop(0, rows, one_row, 0)
            src, dst = dst, src
        back.append(send(ready[g], outs[g], 1 + G + g))
    for sent in back:
        arrive(sent)
    for sent in [sent_a] + sent_b + back:
        for c in sent[0]:
            c.wait_send()


def dedisperse(p, delays, spectra):
    G, parts = p.groups, p.parts
    out_shape = jax.ShapeDtypeStruct((parts, p.per * p.out_blocks, LANES), jnp.float32)
    here = pl.BlockSpec(memory_space=pl.ANY)
    f32 = jnp.float32
    turns = 1 + 2 * G
    return pl.pallas_call(
        functools.partial(tree_kernel, p),
        out_shape=[out_shape] * G,
        in_specs=[pl.BlockSpec(memory_space=SMEM), here],
        out_specs=[here] * G,
        scratch_shapes=[
            pltpu.VMEM((p.rows, p.span), f32),
            pltpu.VMEM((p.rows, p.lead_blocks * LANES), f32),
        ]
        + [pltpu.VMEM((p.rows * p.pitch_a + SUB, LANES), f32)] * 2
        + [pltpu.VMEM((p.rows * p.pitch_b + SUB, LANES), f32)] * 2
        + [pltpu.VMEM((parts, p.own * p.blocks_a, LANES), f32)]
        + [pltpu.VMEM((parts, p.per * p.blocks_b, LANES), f32)] * G
        + [pltpu.VMEM((parts, p.own * p.blocks_a, LANES), f32)]
        + [pltpu.VMEM((parts, p.per * p.blocks_b, LANES), f32)] * G
        + [pltpu.VMEM((parts, p.per * p.out_blocks, LANES), f32)] * G
        + [pltpu.VMEM((p.bands * p.per * p.pitch_x + SUB, LANES), f32)] * 2
        + [
            pltpu.SemaphoreType.DMA((2, turns, parts)),
            pltpu.SemaphoreType.DMA((turns,)),
            pltpu.SemaphoreType.DMA((2,)),
            pltpu.SemaphoreType.DMA((2,)),
        ],
        compiler_params=pltpu.CompilerParams(
            collective_id=0, has_side_effects=True, vmem_limit_bytes=40 << 20
        ),
    )(delays, spectra)


def filter_kernel(p, filters, parts, per_dot, widths, *refs):
    G = p.groups
    xs, (out, matrix, lhs) = refs[:G], refs[G:]
    rows = parts * p.per
    stride = p.out_blocks

    @pl.when(pl.program_id(0) == 0)
    def _():
        pos = lax.broadcasted_iota(jnp.int32, (2 * TAPS, TAPS), 0)
        dist = pos - lax.broadcasted_iota(jnp.int32, (2 * TAPS, TAPS), 1)
        for w in range(filters):
            box = (dist >= 0) & (dist < widths[w])
            value = jnp.where(box, 1.0, 0.0).astype(jnp.bfloat16)
            for n in range(2):
                matrix[n * 2 * TAPS : (n + 1) * 2 * TAPS, w * TAPS : (w + 1) * TAPS] = value

    for g, x in enumerate(xs):
        for n in range(p.blocks + 1):
            v = x[pl.ds(n, rows, stride=stride), :]
            h = v.astype(jnp.bfloat16)
            t = (v - h.astype(jnp.float32)).astype(jnp.bfloat16)
            for k, part in enumerate((h, h, t, t)):
                at = ((n - k % 2) * G + g) * rows
                if 0 <= n - k % 2 < p.blocks:
                    lhs[at : at + rows, k * LANES : (k + 1) * LANES] = part

    together = 2 if filters % 2 == 0 else 1
    for w in range(0, filters, together):
        m = matrix[:, w * TAPS : (w + together) * TAPS]
        scale = [
            1.0 / jnp.sqrt(jnp.full((SUB, LANES), widths[w + n], jnp.int32).astype(jnp.float32) * p.all_rows)
            for n in range(together)
        ]
        for first in range(0, p.blocks, per_dot):
            size = per_dot * G * rows
            y = jnp.dot(
                lhs[first * G * rows : first * G * rows + size, :], m, preferred_element_type=jnp.float32
            )
            for b in range(per_dot):
                at = (first + b) * LANES
                for g in range(G):
                    low = (b * G + g) * rows
                    for n in range(together):
                        part = y[low : low + rows, n * TAPS : (n + 1) * TAPS]
                        part = part * scale[n][:1]
                        shape = (out.shape[1], out.shape[2] // G, LANES)
                        out[w + n, :, g * shape[1] : (g + 1) * shape[1], at : at + LANES] = part.reshape(shape)


def filter_rows(p, xs, widths):
    filters = widths.shape[0]
    if p.per % SUB:
        parts, view = p.parts, (filters, 1, p.parts * p.own, p.span)
        block = view
    else:
        parts = 2 if p.parts % 2 == 0 else 1
        view = (filters, p.parts, p.own, p.span)
        block = (filters, parts, p.own, p.span)
    per_dot = 4 if p.blocks % 4 == 0 else 1
    rows = parts * p.per * p.out_blocks
    cells = filters * p.rows * p.span
    return pl.pallas_call(
        functools.partial(filter_kernel, p, filters, parts, per_dot),
        grid=(p.parts // parts,),
        out_shape=jax.ShapeDtypeStruct(view, jnp.float32),
        in_specs=[pl.BlockSpec(memory_space=SMEM)]
        + [pl.BlockSpec((rows, LANES), lambda s: (s, 0))] * p.groups,
        out_specs=pl.BlockSpec(block, lambda s: (0, s, 0, 0)),
        scratch_shapes=[
            pltpu.VMEM((4 * TAPS, filters * TAPS), jnp.bfloat16),
            pltpu.VMEM((p.blocks * p.groups * parts * p.per, 4 * TAPS), jnp.bfloat16),
        ],
        compiler_params=pltpu.CompilerParams(vmem_limit_bytes=40 << 20),
        cost_estimate=pl.CostEstimate(flops=1024 * cells, bytes_accessed=4 * cells, transcendentals=0),
    )(widths, *xs)


GROUPS = 2


def local(spectra, delays, widths):
    rows, span = spectra.shape
    p = Plan(rows, span, *delays.shape, lax.axis_size("freq"), lax.axis_size("tm"), GROUPS)
    xs = dedisperse(p, delays, spectra)
    xs = [x.reshape(-1, LANES) for x in xs]
    return filter_rows(p, xs, widths).reshape(widths.shape[0], rows, span)


def solution(mesh):
    return jax.shard_map(
        local,
        mesh=mesh,
        in_specs=(P(("beam", "freq"), "tm"), P(), P()),
        out_specs=P(None, ("beam", "freq"), "tm"),
        check_vma=False,
    )
```

time: 168 us -> 155 us (0.923)
  the two profiles are of different devices: /device:TPU:15 before, /device:TPU:0 now
where the time goes in v1:
time: 155 us; the launch traced here: 154 us
  Pallas kernels  152 us (98%)
  local copies, waits for them, and re-layouts  2.65 us (2%)
    pallas_call x1, Pallas kernels, dedisperse(): pl.pallas_call(functools.partial(tree_kernel, p), out_shape=[out_shape] *...  140 us
    pallas_call x1, Pallas kernels, filter_rows(): pl.pallas_call(functools.partial(filter_kernel, p, filters, parts, per_do...  11.5 us

profile of v1, /device:TPU:0, one launch (start us, length us, event | category | flops | bytes accessed | tf_op | source)
XLA Modules:
  0.0 154.5 jit_solution(500248848501530102)
XLA Ops:
  0.0 0.0 copy-start
  0.0 1.7 %copy-done = f32[256,2560]{1,0:T(8,128)S(1)} copy-done((f32[256,2560]{1,0:T(8,128)S(1)}, f32[256,2560]{1,0:T(8,128)}, u32[]{:S(2)}) %copy-start) | copy-done | bytes 2621464
  1.7 0.0 copy-start.1
  1.7 0.9 copy-done.1
  2.6 0.0 copy-start.2
  2.6 140.3 %shard_map.37 = (f32[16,168,128]{2,1,0:T(8,128)S(1)}, f32[16,168,128]{2,1,0:T(8,128)S(1)}) custom-call(s32[11,2048]{1,0:T(8,128)S(1)} %copy-done.1, f32[256,2560]{1,0:T(8,128)S(1)} %copy-done), custom_call_target="tpu_custom_call" | custom-call | tf_op jit(solution)/shard_map/pallas_call | solution.py:285
  143.0 0.0 copy-done.2
  143.0 11.5 %shard_map.38 = f32[8,16,16,2560]{3,2,1,0:T(8,128)} custom-call(s32[8]{0:T(128)S(1)} %copy-done.2, f32[2688,128]{1,0:T(8,128)S(1)} %bitcast.3, f32[2688,128]{1,0:T(8,128)S(1)} %bitcast.4), custom_call_target="tpu_custom_call" | custom-call | flops 5368709120 | bytes 20971520 | tf_op jit(solution)/shard_map/pallas_call | solution.py:375
Async XLA Ops:
  0.0 1.7 %copy-start = (f32[256,2560]{1,0:T(8,128)S(1)}, f32[256,2560]{1,0:T(8,128)}, u32[]{:S(2)}) copy-start(f32[256,2560]{1,0:T(8,128)} %spectra.1) | copy-start | bytes 7864324
  1.7 0.9 copy-start.1
  2.6 140.3 %copy-start.2 = (s32[8]{0:T(128)S(1)}, s32[8]{0:T(128)}, u32[]{:S(2)}) copy-start(s32[8]{0:T(128)} %widths.1) | copy-start | bytes 100

commit v2 on v1

v2 whole, which is shorter than its diff:
```python
import functools

import jax
import jax.numpy as jnp
from jax import lax
from jax.experimental import pallas as pl
from jax.experimental.pallas import tpu as pltpu
from jax.sharding import PartitionSpec as P

LANES = 128
SUB = 8
VMEM = pltpu.MemorySpace.VMEM
SMEM = pltpu.MemorySpace.SMEM
MESH = pl.DeviceIdType.MESH


def cdiv(a, b):
    return -(-a // b)


def round_up(a, b):
    return cdiv(a, b) * b


def shifted(src, start, width, shift, lane):
    start = start + lax.shift_right_logical(shift, LANES.bit_length() - 1)
    shift = shift & (LANES - 1)
    low = src[pl.ds(start, width), :]
    high = src[pl.ds(start + 1, width), :]
    return pltpu.roll(jnp.where(lane < shift, high, low), LANES - shift, 1)


class Plan:
    def __init__(self, rows, span, all_levels, all_rows, bands, halves, groups):
        self.rows, self.span = rows, span
        self.all_levels, self.all_rows = all_levels, all_rows
        self.levels = rows.bit_length() - 1
        self.bits = all_levels - self.levels
        self.bands, self.halves = bands, halves
        self.parts = bands * halves
        self.own = rows // self.parts
        self.groups = groups if self.own % (SUB * groups) == 0 else 1
        self.per = self.own // self.groups
        self.blocks = span // LANES
        self.lead_blocks = cdiv(rows - 1, LANES)
        self.blocks_a = SUB - self.lead_blocks
        self.blocks_b = self.blocks - self.blocks_a
        self.pitch_a = SUB
        self.pitch_b = round_up(self.blocks_b + self.lead_blocks, SUB)
        self.total = self.blocks * halves
        reach = 2 ** (all_levels - 1)
        self.pitch_x = round_up(self.total + cdiv(reach, LANES) + 2, SUB)
        starts = list(range(0, self.levels, 3))
        self.passes = [(first, min(3, self.levels - first)) for first in starts]
        assert rows <= 2 * LANES and 2 ** self.passes[-1][0] >= self.own
        self.window = max(rows, LANES)


def tree_kernel(plan, delays, spectra, *refs):
    p = plan
    G, parts, halves, bands = p.groups, p.parts, p.halves, p.bands
    refs = list(refs)

    def take(n):
        got = refs[:n]
        del refs[:n]
        return got

    outs, edges = take(G), take(G)
    (rows_in, lead) = take(2)
    tree_a, tree_b = take(2), take(2)
    (send_a,) = take(1)
    send_b = take(G)
    (came_a,) = take(1)
    came_b = take(G)
    ready, ready_edge = take(G), take(G)
    buf_a, buf_b = take(2)
    own_delays, band_delays = take(2)
    sems, edge_sems, own_sems, in_sems, lead_sems, band_sems = take(6)

    beam, freq, tm = (lax.axis_index(n) for n in ("beam", "freq", "tm"))
    me = freq * halves + tm
    head = SUB * LANES

    load_a = pltpu.make_async_copy(spectra.at[:, :head], rows_in.at[:, :head], in_sems.at[0])
    load_b = pltpu.make_async_copy(spectra.at[:, head:], rows_in.at[:, head:], in_sems.at[1])
    own_first = freq * p.rows // p.window * p.window
    own_at = freq * p.rows - own_first
    load_own = pltpu.make_async_copy(
        delays.at[:, pl.ds(pl.multiple_of(own_first, LANES), p.window)], own_delays, in_sems.at[2]
    )
    load_bands = []
    for j in range(bands):
        at = (j * p.rows + me * p.own) // LANES * LANES
        load_bands.append(
            pltpu.make_async_copy(
                delays.at[:, pl.ds(pl.multiple_of(at, LANES), LANES)], band_delays.at[j], band_sems.at[j]
            )
        )
    load_a.start()
    load_own.start()
    load_b.start()
    for c in load_bands:
        c.start()

    def peer(k):
        other = me
        step = 1
        while step < parts:
            if k & step:
                other = other + step * (1 - 2 * ((me // step) % 2))
            step *= 2
        return other, (beam, other // halves, other % halves)

    barrier = pltpu.get_barrier_semaphore()
    for k in range(1, parts):
        pl.semaphore_signal(barrier, inc=1, device_id=peer(k)[1], device_id_type=MESH)

    def spread(buf, pitch, first, count, lead_count):
        def body(n, carry):
            at = pl.ds(pl.multiple_of(n * SUB, SUB), SUB)
            for b in range(count):
                v = rows_in[at, (first + b) * LANES : (first + b + 1) * LANES]
                buf[pl.ds(n * (SUB * pitch) + b, SUB, stride=pitch), :] = v
            for b in range(lead_count):
                v = lead[at, b * LANES : (b + 1) * LANES]
                v = jnp.where(tm < halves - 1, v, 0.0)
                buf[pl.ds(n * (SUB * pitch) + count + b, SUB, stride=pitch), :] = v
            return carry

        lax.fori_loop(0, p.rows // SUB, body, 0)

    def several(src, pitch, first, depth, base, put):
        lane = lax.broadcasted_iota(jnp.int32, (pitch, LANES), 1)
        half = 2**first
        rows = [src[pl.ds(pl.multiple_of((base + m * half) * pitch, SUB), pitch), :] for m in range(2**depth)]
        for t in range(depth):
            step = 2**t
            for m in range(2**depth):
                if m & step:
                    continue
                a, low = rows[m], rows[m + step]
                high = pltpu.roll(low, pitch - 1, 0)
                for q in (m, m + step):
                    shift = own_delays[first + t, own_at + base + q * half]
                    rows[q] = a + pltpu.roll(jnp.where(lane < shift, high, low), LANES - shift, 1)
        for m, v in enumerate(rows):
            put(base + m * half, v)

    def levels(bufs, pitch, together):
        src, dst = bufs
        for first, depth in p.passes[:-1]:
            count = p.rows >> depth

            def body(n, carry, src=src, dst=dst, first=first, depth=depth):
                def put(row, v):
                    dst[pl.ds(pl.multiple_of(row * pitch, SUB), pitch), :] = v

                for u in range(together):
                    q = n * together + u
                    base = ((q >> first) << (first + depth)) + (q & (2**first - 1))
                    several(src, pitch, first, depth, base, put)
                return carry

            lax.fori_loop(0, count // together, body, 0)
            src, dst = dst, src
        return src

    def last_levels(src, pitch, out, blocks, group, per, together):
        first, depth = p.passes[-1]
        per_bits, own_bits = per.bit_length() - 1, p.own.bit_length() - 1
        count = (p.rows >> depth) * per // p.own

        def body(n, carry):
            for u in range(together):
                q = n * together + u
                base = ((q >> per_bits) << own_bits) + group * per + (q & (per - 1))
                at = (q & (per - 1)) * blocks

                def put(row, v):
                    out[row >> own_bits, pl.ds(at, blocks), :] = v[:blocks]

                several(src, pitch, first, depth, base, put)
            return carry

        lax.fori_loop(0, count // together, body, 0)

    def send(src, dst, turn):
        copies = []
        for k in range(parts - 1, 0, -1):
            other, where = peer(k)
            c = pltpu.make_async_remote_copy(
                src_ref=src.at[other],
                dst_ref=dst.at[me],
                send_sem=sems.at[0, turn, k],
                recv_sem=sems.at[1, turn, k],
                device_id=where,
                device_id_type=MESH,
            )
            c.start()
            copies.append(c)
        c = pltpu.make_async_copy(src.at[me], dst.at[me], own_sems.at[turn])
        c.start()
        return copies, c

    def send_edges(src, dst, turn):
        copies = []
        for k in range(parts - 1, 0, -1):
            other, where = peer(k)
            c = pltpu.make_async_remote_copy(
                src_ref=src.at[other],
                dst_ref=dst.at[me],
                send_sem=edge_sems.at[0, turn, k],
                recv_sem=edge_sems.at[1, turn, k],
                device_id=where,
                device_id_type=MESH,
            )

            @pl.when(other % halves < halves - 1)
            def _(c=c):
                c.start()

            copies.append((other, c))
        c = pltpu.make_async_copy(src.at[me], dst.at[me], own_sems.at[1 + 2 * G + turn])

        @pl.when(tm < halves - 1)
        def _(c=c):
            c.start()

        return copies, c

    def arrive(sent):
        for c in sent[0]:
            c.wait_recv()
        sent[1].wait()

    load_a.wait()
    spread(tree_a[0], p.pitch_a, 0, SUB, 0)
    load_own.wait()
    src = levels(tree_a, p.pitch_a, 2)
    last_levels(src, p.pitch_a, send_a, p.blocks_a, 0, p.own, 2)

    pl.semaphore_wait(barrier, parts - 1)
    left = (tm + halves - 1) % halves
    get_lead = pltpu.make_async_remote_copy(
        src_ref=spectra.at[:, : p.lead_blocks * LANES],
        dst_ref=lead,
        send_sem=lead_sems.at[0],
        recv_sem=lead_sems.at[1],
        device_id=(beam, freq, left),
        device_id_type=MESH,
    )
    get_lead.start()
    sent_a = send(send_a, came_a, 0)

    load_b.wait()
    get_lead.wait()
    spread(tree_b[0], p.pitch_b, p.blocks_a, p.blocks_b, p.lead_blocks)
    src = levels(tree_b, p.pitch_b, 1)
    sent_b = []
    for g in range(G):
        last_levels(src, p.pitch_b, send_b[g], p.blocks_b, g, p.per, 1)
        sent_b.append(send(send_b[g], came_b[g], 1 + g))

    total, pitch, rows = p.total, p.pitch_x, p.per
    lane = lax.broadcasted_iota(jnp.int32, (total, LANES), 1)
    zero = jnp.zeros((pitch - total, LANES), jnp.float32)

    def clear(r, carry):
        for buf in (buf_a, buf_b):
            buf[pl.ds(r * pitch + total, pitch - total), :] = zero
        return carry

    lax.fori_loop(0, bands * rows, clear, 0)
    for buf in (buf_a, buf_b):
        buf[pl.ds(bands * rows * pitch, SUB), :] = jnp.zeros((SUB, LANES), jnp.float32)

    back, back_edges = [], []
    for c in load_bands:
        c.wait()
    arrive(sent_a)
    for g in range(G):
        arrive(sent_b[g])

        def gather(i, carry, g=g):
            for s in range(bands):
                at = (s * rows + i) * pitch
                for c in range(halves):
                    piece = came_a[s * halves + c, pl.ds((g * rows + i) * p.blocks_a, p.blocks_a), :]
                    buf_a[pl.ds(at + c * p.blocks, p.blocks_a), :] = piece
                    piece = came_b[g][s * halves + c, pl.ds(i * p.blocks_b, p.blocks_b), :]
                    buf_a[pl.ds(at + c * p.blocks + p.blocks_a, p.blocks_b), :] = piece
            return carry

        lax.fori_loop(0, rows, gather, 0)

        src, dst = buf_a, buf_b
        for level in range(p.bits):
            step = 2**level

            def one_row(i, carry, src=src, dst=dst, step=step, level=level, g=g):
                for j in range(bands):
                    base = (j // (2 * step)) * (2 * step) + j % step
                    at = (j * p.rows + me * p.own) % LANES + g * rows + i
                    shift = band_delays[j, p.levels + level, at]
                    at_a = pl.multiple_of((base * rows + i) * pitch, SUB)
                    at_b = pl.multiple_of(((base + step) * rows + i) * pitch, SUB)
                    if level < p.bits - 1:
                        a = src[pl.ds(at_a, total), :]
                        at = pl.multiple_of((j * rows + i) * pitch, SUB)
                        dst[pl.ds(at, total), :] = a + shifted(src, at_b, total, shift, lane)
                        continue
                    v = src[pl.ds(at_a, total), :] + shifted(src, at_b, total, shift, lane)
                    for c in range(halves):
                        first = c * p.blocks
                        ready[g][j * halves + c, pl.ds(i * p.blocks, p.blocks), :] = v[first : first + p.blocks]
                        if c > 0:
                            ready_edge[g][j * halves + c - 1, pl.ds(i, 1), :] = v[first : first + 1]
                return carry

            lax.fori_loop(0, rows, one_row, 0)
            src, dst = dst, src
        back.append(send(ready[g], outs[g], 1 + G + g))
        back_edges.append(send_edges(ready_edge[g], edges[g], g))
    for sent, (copies, c) in zip(back, back_edges):
        arrive(sent)

        @pl.when(tm < halves - 1)
        def _(copies=copies, c=c):
            for other, remote in copies:
                remote.wait_recv()
            c.wait()

    for sent in [sent_a] + sent_b + back:
        for c in sent[0]:
            c.wait_send()
    for copies, _ in back_edges:
        for other, remote in copies:

            @pl.when(other % halves < halves - 1)
            def _(remote=remote):
                remote.wait_send()


def dedisperse(p, delays, spectra):
    G, parts = p.groups, p.parts
    out_shape = jax.ShapeDtypeStruct((parts, p.per * p.blocks, LANES), jnp.float32)
    edge_shape = jax.ShapeDtypeStruct((parts, p.per, LANES), jnp.float32)
    here = pl.BlockSpec(memory_space=pl.ANY)
    f32 = jnp.float32
    turns = 1 + 2 * G
    return pl.pallas_call(
        functools.partial(tree_kernel, p),
        out_shape=[out_shape] * G + [edge_shape] * G,
        in_specs=[pl.BlockSpec(memory_space=pltpu.MemorySpace.HBM)] * 2,
        out_specs=[here] * (2 * G),
        scratch_shapes=[
            pltpu.VMEM((p.rows, p.span), f32),
            pltpu.VMEM((p.rows, p.lead_blocks * LANES), f32),
        ]
        + [pltpu.VMEM((p.rows * p.pitch_a + SUB, LANES), f32)] * 2
        + [pltpu.VMEM((p.rows * p.pitch_b + SUB, LANES), f32)] * 2
        + [pltpu.VMEM((parts, p.own * p.blocks_a, LANES), f32)]
        + [pltpu.VMEM((parts, p.per * p.blocks_b, LANES), f32)] * G
        + [pltpu.VMEM((parts, p.own * p.blocks_a, LANES), f32)]
        + [pltpu.VMEM((parts, p.per * p.blocks_b, LANES), f32)] * G
        + [pltpu.VMEM((parts, p.per * p.blocks, LANES), f32)] * G
        + [pltpu.VMEM((parts, p.per, LANES), f32)] * G
        + [pltpu.VMEM((p.bands * p.per * p.pitch_x + SUB, LANES), f32)] * 2
        + [
            pltpu.SMEM((p.all_levels, p.window), jnp.int32),
            pltpu.SMEM((p.bands, p.all_levels, LANES), jnp.int32),
            pltpu.SemaphoreType.DMA((2, turns, parts)),
            pltpu.SemaphoreType.DMA((2, G, parts)),
            pltpu.SemaphoreType.DMA((turns + G,)),
            pltpu.SemaphoreType.DMA((3,)),
            pltpu.SemaphoreType.DMA((2,)),
            pltpu.SemaphoreType.DMA((p.bands,)),
        ],
        compiler_params=pltpu.CompilerParams(
            collective_id=0, has_side_effects=True, vmem_limit_bytes=58 << 20
        ),
    )(delays, spectra)


def filter_kernel(p, filters, parts, widths, *refs):
    G = p.groups
    xs, edges, (out, matrix, lhs, sums) = refs[:G], refs[G : 2 * G], refs[2 * G :]
    rows = parts * p.per
    size = G * rows
    last = lax.axis_index("tm") == p.halves - 1

    @pl.when(pl.program_id(0) == 0)
    def _():
        source = lax.broadcasted_iota(jnp.int32, (LANES, LANES), 0)
        target = lax.broadcasted_iota(jnp.int32, (LANES, LANES), 1)
        for k, taken in enumerate((source <= target, source < LANES)):
            value = jnp.where(taken, 1.0, 0.0).astype(jnp.bfloat16)
            for n in range(2):
                matrix[n * LANES : (n + 1) * LANES, k * LANES : (k + 1) * LANES] = value

    for g in range(G):
        for n in range(p.blocks + 1):
            if n < p.blocks:
                v = xs[g][pl.ds(n, rows, stride=p.blocks), :]
            else:
                v = jnp.where(last, 0.0, edges[g][...])
            h = v.astype(jnp.bfloat16)
            t = (v - h.astype(jnp.float32)).astype(jnp.bfloat16)
            at = n * size + g * rows
            lhs[at : at + rows, :LANES] = h
            lhs[at : at + rows, LANES:] = t
    sums[...] = jnp.dot(lhs[...], matrix[...], preferred_element_type=jnp.float32)

    lane = lax.broadcasted_iota(jnp.int32, (size, LANES), 1)
    scale = []
    for w in range(filters):
        width = jnp.full((size, LANES), widths[w], jnp.int32).astype(jnp.float32)
        scale.append(1.0 / jnp.sqrt(width * p.all_rows))
    for n in range(p.blocks):
        here = slice(n * size, (n + 1) * size)
        low = sums[here, :LANES]
        high = sums[here, LANES:] + sums[(n + 1) * size : (n + 2) * size, :LANES]
        x = [xs[g][pl.ds(n, rows, stride=p.blocks), :] for g in range(G)]
        before = low - jnp.concatenate(x, axis=0)
        for w in range(filters):
            shift = widths[w] - 1
            upto = pltpu.roll(jnp.where(lane < shift, high, low), LANES - shift, 1)
            y = (upto - before) * scale[w]
            for g in range(G):
                shape = (out.shape[1], out.shape[2] // G, LANES)
                rows_out = slice(g * shape[1], (g + 1) * shape[1])
                out[w, :, rows_out, n * LANES : (n + 1) * LANES] = y[g * rows : (g + 1) * rows].reshape(shape)


def filter_rows(p, xs, edges, widths):
    filters = widths.shape[0]
    if p.per % SUB:
        parts, view = p.parts, (filters, 1, p.parts * p.own, p.span)
        block = view
    else:
        parts = PARTS if p.parts % PARTS == 0 else 1
        view = (filters, p.parts, p.own, p.span)
        block = (filters, parts, p.own, p.span)
    rows = parts * p.per
    total = rows * p.groups * (p.blocks + 1)
    cells = filters * p.rows * p.span
    return pl.pallas_call(
        functools.partial(filter_kernel, p, filters, parts),
        grid=(p.parts // parts,),
        out_shape=jax.ShapeDtypeStruct(view, jnp.float32),
        in_specs=[pl.BlockSpec(memory_space=SMEM)]
        + [pl.BlockSpec((rows * p.blocks, LANES), lambda s: (s, 0))] * p.groups
        + [pl.BlockSpec((rows, LANES), lambda s: (s, 0))] * p.groups,
        out_specs=pl.BlockSpec(block, lambda s: (0, s, 0, 0)),
        scratch_shapes=[
            pltpu.VMEM((2 * LANES, 2 * LANES), jnp.bfloat16),
            pltpu.VMEM((total, 2 * LANES), jnp.bfloat16),
            pltpu.VMEM((total, 2 * LANES), jnp.float32),
        ],
        compiler_params=pltpu.CompilerParams(vmem_limit_bytes=58 << 20),
        cost_estimate=pl.CostEstimate(flops=96 * cells, bytes_accessed=4 * cells, transcendentals=0),
    )(widths, *xs, *edges)


PARTS = 4
GROUPS = 2


def local(spectra, delays, widths):
    rows, span = spectra.shape
    p = Plan(rows, span, *delays.shape, lax.axis_size("freq"), lax.axis_size("tm"), GROUPS)
    made = [x.reshape(-1, LANES) for x in dedisperse(p, delays, spectra)]
    out = filter_rows(p, made[: p.groups], made[p.groups :], widths)
    return out.reshape(widths.shape[0], rows, span)


def solution(mesh):
    return jax.shard_map(
        local,
        mesh=mesh,
        in_specs=(P(("beam", "freq"), "tm"), P(), P()),
        out_specs=P(None, ("beam", "freq"), "tm"),
        check_vma=False,
    )
```

time: 155 us -> 153 us (0.987)
  local copies, waits for them, and re-layouts: 2.65 us -> 0 us
    unnamed x6 -> x0, local copies, waits for them, and re-layouts: 2.65 us -> none
where the time goes in v2:
time: 153 us
  Pallas kernels  153 us (100%)
    pallas_call x1, Pallas kernels, dedisperse(): pl.pallas_call(functools.partial(tree_kernel, p), out_shape=[out_shape] *...  142 us
    pallas_call x1, Pallas kernels, filter_rows(): pl.pallas_call(functools.partial(filter_kernel, p, filters, parts), grid=...  11.1 us

profile of v2, /device:TPU:0, one launch (start us, length us, event | category | flops | bytes accessed | tf_op | source)
XLA Modules:
  0.0 152.9 jit_solution(9739859665927114342)
XLA Ops:
  0.0 141.8 %shard_map.37 = (f32[16,160,128]{2,1,0:T(8,128)}, f32[16,160,128]{2,1,0:T(8,128)}, f32[16,8,128]{2,1,0:T(8,128)}, f32[16,8,128]{2,1,0:T(8,128)}) custom-call(s32[11,2048]{1,0:T(8,128)} %delays.1, f32[256,2560]{1,0:T(8,128)} %spectra.1), custom_call_target="tpu_custom_call" | custom-call | tf_op jit(solution)/shard_map/pallas_call | solution.py:352
  141.8 11.1 %shard_map.38 = f32[8,16,16,2560]{3,2,1,0:T(8,128)} custom-call(s32[8]{0:T(128)} %widths.1, f32[2560,128]{1,0:T(8,128)} %bitcast.5, f32[2560,128]{1,0:T(8,128)} %bitcast.6, f32[128,128]{1,0:T(8,128)} %bitcast.7, f32[128,128]{1,0:T(8,128)} %bitcast.8), custom_call_target="tpu_custom_call" | custom-call | flops 503316480 | bytes 20971520 | tf_op jit(solution)/shard_map/pallas_call | solution.py:448

commit v3 on v2

--- a/solution.py
+++ b/solution.py
@@ -151,18 +151,19 @@
         src, dst = bufs
         for first, depth in p.passes[:-1]:
             count = p.rows >> depth
-
-            def body(n, carry, src=src, dst=dst, first=first, depth=depth):
+            unroll = min(together, count)
+
+            def body(n, carry, src=src, dst=dst, first=first, depth=depth, unroll=unroll):
                 def put(row, v):
                     dst[pl.ds(pl.multiple_of(row * pitch, SUB), pitch), :] = v
 
-                for u in range(together):
-                    q = n * together + u
+                for u in range(unroll):
+                    q = n * unroll + u
                     base = ((q >> first) << (first + depth)) + (q & (2**first - 1))
                     several(src, pitch, first, depth, base, put)
                 return carry
 
-            lax.fori_loop(0, count // together, body, 0)
+            lax.fori_loop(0, count // unroll, body, 0)
             src, dst = dst, src
         return src
 
@@ -170,10 +171,11 @@
         first, depth = p.passes[-1]
         per_bits, own_bits = per.bit_length() - 1, p.own.bit_length() - 1
         count = (p.rows >> depth) * per // p.own
+        unroll = min(together, count)
 
         def body(n, carry):
-            for u in range(together):
-                q = n * together + u
+            for u in range(unroll):
+                q = n * unroll + u
                 base = ((q >> per_bits) << own_bits) + group * per + (q & (per - 1))
                 at = (q & (per - 1)) * blocks
 
@@ -183,7 +185,7 @@
                 several(src, pitch, first, depth, base, put)
             return carry
 
-        lax.fori_loop(0, count // together, body, 0)
+        lax.fori_loop(0, count // unroll, body, 0)
 
     def send(src, dst, turn):
         copies = []
@@ -237,8 +239,8 @@
     load_a.wait()
     spread(tree_a[0], p.pitch_a, 0, SUB, 0)
     load_own.wait()
-    src = levels(tree_a, p.pitch_a, 2)
-    last_levels(src, p.pitch_a, send_a, p.blocks_a, 0, p.own, 2)
+    src = levels(tree_a, p.pitch_a, 8)
+    last_levels(src, p.pitch_a, send_a, p.blocks_a, 0, p.own, 8)
 
     pl.semaphore_wait(barrier, parts - 1)
     left = (tm + halves - 1) % halves
@@ -256,10 +258,10 @@
     load_b.wait()
     get_lead.wait()
     spread(tree_b[0], p.pitch_b, p.blocks_a, p.blocks_b, p.lead_blocks)
-    src = levels(tree_b, p.pitch_b, 1)
+    src = levels(tree_b, p.pitch_b, 4)
     sent_b = []
     for g in range(G):
-        last_levels(src, p.pitch_b, send_b[g], p.blocks_b, g, p.per, 1)
+        last_levels(src, p.pitch_b, send_b[g], p.blocks_b, g, p.per, 4)
         sent_b.append(send(send_b[g], came_b[g], 1 + g))
 
     total, pitch, rows = p.total, p.pitch_x, p.per

time: 153 us -> 141 us (0.922)
  Pallas kernels: 153 us -> 141 us
    pallas_call x1, Pallas kernels: 142 us -> 130 us  [dedisperse(): pl.pallas_call(functools.partial(tree_kernel, p), out_shape=[out_shape] *...]
where the time goes in v3:
time: 141 us
  Pallas kernels  141 us (100%)
    pallas_call x1, Pallas kernels, dedisperse(): pl.pallas_call(functools.partial(tree_kernel, p), out_shape=[out_shape] *...  130 us
    pallas_call x1, Pallas kernels, filter_rows(): pl.pallas_call(functools.partial(filter_kernel, p, filters, parts), grid=...  11.1 us

profile of v3, /device:TPU:0, one launch (start us, length us, event | category | flops | bytes accessed | tf_op | source)
XLA Modules:
  0.0 140.9 jit_solution(14630925605790885264)
XLA Ops:
  0.0 129.8 %shard_map.37 = (f32[16,160,128]{2,1,0:T(8,128)}, f32[16,160,128]{2,1,0:T(8,128)}, f32[16,8,128]{2,1,0:T(8,128)}, f32[16,8,128]{2,1,0:T(8,128)}) custom-call(s32[11,2048]{1,0:T(8,128)} %delays.1, f32[256,2560]{1,0:T(8,128)} %spectra.1), custom_call_target="tpu_custom_call" | custom-call | tf_op jit(solution)/shard_map/pallas_call | solution.py:354
  129.9 11.1 %shard_map.38 = f32[8,16,16,2560]{3,2,1,0:T(8,128)} custom-call(s32[8]{0:T(128)} %widths.1, f32[2560,128]{1,0:T(8,128)} %bitcast.5, f32[2560,128]{1,0:T(8,128)} %bitcast.6, f32[128,128]{1,0:T(8,128)} %bitcast.7, f32[128,128]{1,0:T(8,128)} %bitcast.8), custom_call_target="tpu_custom_call" | custom-call | flops 503316480 | bytes 20971520 | tf_op jit(solution)/shard_map/pallas_call | solution.py:450

commit v4 on v3

--- a/solution.py
+++ b/solution.py
@@ -28,6 +28,16 @@
     low = src[pl.ds(start, width), :]
     high = src[pl.ds(start + 1, width), :]
     return pltpu.roll(jnp.where(lane < shift, high, low), LANES - shift, 1)
+
+
+def flipped(me, k, parts):
+    other = me
+    step = 1
+    while step < parts:
+        if k & step:
+            other = other + step * (1 - 2 * ((me // step) % 2))
+        step *= 2
+    return other
 
 
 class Plan:
@@ -50,6 +60,8 @@
         self.total = self.blocks * halves
         reach = 2 ** (all_levels - 1)
         self.pitch_x = round_up(self.total + cdiv(reach, LANES) + 2, SUB)
+        self.relays = RELAYS if self.groups > 1 and self.parts >= 2 * RELAYS else 0
+        self.far = self.parts // 2
         starts = list(range(0, self.levels, 3))
         self.passes = [(first, min(3, self.levels - first)) for first in starts]
         assert rows <= 2 * LANES and 2 ** self.passes[-1][0] >= self.own
@@ -67,6 +79,7 @@
         return got
 
     outs, edges = take(G), take(G)
+    relay = take(1)[0] if p.relays else None
     (rows_in, lead) = take(2)
     tree_a, tree_b = take(2), take(2)
     (send_a,) = take(1)
@@ -76,7 +89,7 @@
     ready, ready_edge = take(G), take(G)
     buf_a, buf_b = take(2)
     own_delays, band_delays = take(2)
-    sems, edge_sems, own_sems, in_sems, lead_sems, band_sems = take(6)
+    sems, edge_sems, own_sems, in_sems, lead_sems, band_sems, relay_sems = take(7)
 
     beam, freq, tm = (lax.axis_index(n) for n in ("beam", "freq", "tm"))
     me = freq * halves + tm
@@ -104,12 +117,7 @@
         c.start()
 
     def peer(k):
-        other = me
-        step = 1
-        while step < parts:
-            if k & step:
-                other = other + step * (1 - 2 * ((me // step) % 2))
-            step *= 2
+        other = flipped(me, k, parts)
         return other, (beam, other // halves, other % halves)
 
     barrier = pltpu.get_barrier_semaphore()
@@ -187,9 +195,11 @@
 
         lax.fori_loop(0, count // unroll, body, 0)
 
-    def send(src, dst, turn):
+    def send(src, dst, turn, left_out=()):
         copies = []
         for k in range(parts - 1, 0, -1):
+            if k in left_out:
+                continue
             other, where = peer(k)
             c = pltpu.make_async_remote_copy(
                 src_ref=src.at[other],
@@ -205,9 +215,11 @@
         c.start()
         return copies, c
 
-    def send_edges(src, dst, turn):
+    def send_edges(src, dst, turn, left_out=()):
         copies = []
         for k in range(parts - 1, 0, -1):
+            if k in left_out:
+                continue
             other, where = peer(k)
             c = pltpu.make_async_remote_copy(
                 src_ref=src.at[other],
@@ -230,6 +242,27 @@
             c.start()
 
         return copies, c
+
+    def send_relays(src, src_edge):
+        copies = []
+        for k in range(p.relays):
+            other, _ = peer(p.far + k)
+            for n, (x, first, size) in enumerate(((src, 0, p.per * p.blocks), (src_edge, p.per * p.blocks, p.per))):
+                to = relay.at[k, pl.ds(first, size)]
+                if k == 0:
+                    c = pltpu.make_async_copy(x.at[other], to, relay_sems.at[0, n, k])
+                else:
+                    c = pltpu.make_async_remote_copy(
+                        src_ref=x.at[other],
+                        dst_ref=to,
+                        send_sem=relay_sems.at[0, n, k],
+                        recv_sem=relay_sems.at[1, n, k],
+                        device_id=peer(k)[1],
+                        device_id_type=MESH,
+                    )
+                c.start()
+                copies.append(c)
+        return copies
 
     def arrive(sent):
         for c in sent[0]:
@@ -322,8 +355,10 @@
 
             lax.fori_loop(0, rows, one_row, 0)
             src, dst = dst, src
-        back.append(send(ready[g], outs[g], 1 + G + g))
-        back_edges.append(send_edges(ready_edge[g], edges[g], g))
+        left_out = range(p.far, p.far + p.relays) if g == G - 1 else ()
+        back.append(send(ready[g], outs[g], 1 + G + g, left_out))
+        back_edges.append(send_edges(ready_edge[g], edges[g], g, left_out))
+    relayed = send_relays(ready[G - 1], ready_edge[G - 1])
     for sent, (copies, c) in zip(back, back_edges):
         arrive(sent)
 
@@ -333,6 +368,8 @@
                 remote.wait_recv()
             c.wait()
 
+    for c in relayed:
+        c.wait()
     for sent in [sent_a] + sent_b + back:
         for c in sent[0]:
             c.wait_send()
@@ -348,14 +385,17 @@
     G, parts = p.groups, p.parts
     out_shape = jax.ShapeDtypeStruct((parts, p.per * p.blocks, LANES), jnp.float32)
     edge_shape = jax.ShapeDtypeStruct((parts, p.per, LANES), jnp.float32)
+    relay_shapes = []
+    if p.relays:
+        relay_shapes = [jax.ShapeDtypeStruct((p.relays, p.per * (p.blocks + 1), LANES), jnp.float32)]
     here = pl.BlockSpec(memory_space=pl.ANY)
     f32 = jnp.float32
     turns = 1 + 2 * G
     return pl.pallas_call(
         functools.partial(tree_kernel, p),
-        out_shape=[out_shape] * G + [edge_shape] * G,
+        out_shape=[out_shape] * G + [edge_shape] * G + relay_shapes,
         in_specs=[pl.BlockSpec(memory_space=pltpu.MemorySpace.HBM)] * 2,
-        out_specs=[here] * (2 * G),
+        out_specs=[here] * (2 * G + len(relay_shapes)),
         scratch_shapes=[
             pltpu.VMEM((p.rows, p.span), f32),
             pltpu.VMEM((p.rows, p.lead_blocks * LANES), f32),
@@ -378,11 +418,48 @@
             pltpu.SemaphoreType.DMA((3,)),
             pltpu.SemaphoreType.DMA((2,)),
             pltpu.SemaphoreType.DMA((p.bands,)),
+            pltpu.SemaphoreType.DMA((2, 2, max(p.relays, 1))),
         ],
         compiler_params=pltpu.CompilerParams(
             collective_id=0, has_side_effects=True, vmem_limit_bytes=58 << 20
         ),
     )(delays, spectra)
+
+
+def fill_matrix(matrix):
+    source = lax.broadcasted_iota(jnp.int32, (LANES, LANES), 0)
+    target = lax.broadcasted_iota(jnp.int32, (LANES, LANES), 1)
+    for k, taken in enumerate((source <= target, source < LANES)):
+        value = jnp.where(taken, 1.0, 0.0).astype(jnp.bfloat16)
+        for n in range(2):
+            matrix[n * LANES : (n + 1) * LANES, k * LANES : (k + 1) * LANES] = value
+
+
+def prefix_sums(blocks, size, get, matrix, lhs, sums):
+    for n in range(blocks + 1):
+        v = get(n)
+        h = v.astype(jnp.bfloat16)
+        t = (v - h.astype(jnp.float32)).astype(jnp.bfloat16)
+        lhs[n * size : (n + 1) * size, :LANES] = h
+        lhs[n * size : (n + 1) * size, LANES:] = t
+    sums[...] = jnp.dot(lhs[...], matrix[...], preferred_element_type=jnp.float32)
+
+
+def box_ends(n, size, get, sums):
+    low = sums[n * size : (n + 1) * size, :LANES]
+    high = sums[n * size : (n + 1) * size, LANES:] + sums[(n + 1) * size : (n + 2) * size, :LANES]
+    return low, high, low - get(n)
+
+
+def box_scale(width, all_rows, shape):
+    return 1.0 / jnp.sqrt(jnp.full(shape, width, jnp.int32).astype(jnp.float32) * all_rows)
+
+
+def box(ends, width, scale, lane):
+    low, high, before = ends
+    shift = width - 1
+    upto = pltpu.roll(jnp.where(lane < shift, high, low), LANES - shift, 1)
+    return (upto - before) * scale
 
 
 def filter_kernel(p, filters, parts, widths, *refs):
@@ -394,45 +471,88 @@
 
     @pl.when(pl.program_id(0) == 0)
     def _():
-        source = lax.broadcasted_iota(jnp.int32, (LANES, LANES), 0)
-        target = lax.broadcasted_iota(jnp.int32, (LANES, LANES), 1)
-        for k, taken in enumerate((source <= target, source < LANES)):
-            value = jnp.where(taken, 1.0, 0.0).astype(jnp.bfloat16)
-            for n in range(2):
-                matrix[n * LANES : (n + 1) * LANES, k * LANES : (k + 1) * LANES] = value
-
-    for g in range(G):
-        for n in range(p.blocks + 1):
-            if n < p.blocks:
-                v = xs[g][pl.ds(n, rows, stride=p.blocks), :]
-            else:
-                v = jnp.where(last, 0.0, edges[g][...])
-            h = v.astype(jnp.bfloat16)
-            t = (v - h.astype(jnp.float32)).astype(jnp.bfloat16)
-            at = n * size + g * rows
-            lhs[at : at + rows, :LANES] = h
-            lhs[at : at + rows, LANES:] = t
-    sums[...] = jnp.dot(lhs[...], matrix[...], preferred_element_type=jnp.float32)
-
+        fill_matrix(matrix)
+
+    def get(n):
+        if n < p.blocks:
+            return jnp.concatenate([x[pl.ds(n, rows, stride=p.blocks), :] for x in xs], axis=0)
+        return jnp.where(last, 0.0, jnp.concatenate([e[...] for e in edges], axis=0))
+
+    prefix_sums(p.blocks, size, get, matrix, lhs, sums)
     lane = lax.broadcasted_iota(jnp.int32, (size, LANES), 1)
-    scale = []
-    for w in range(filters):
-        width = jnp.full((size, LANES), widths[w], jnp.int32).astype(jnp.float32)
-        scale.append(1.0 / jnp.sqrt(width * p.all_rows))
+    scale = [box_scale(widths[w], p.all_rows, (size, LANES)) for w in range(filters)]
     for n in range(p.blocks):
-        here = slice(n * size, (n + 1) * size)
-        low = sums[here, :LANES]
-        high = sums[here, LANES:] + sums[(n + 1) * size : (n + 2) * size, :LANES]
-        x = [xs[g][pl.ds(n, rows, stride=p.blocks), :] for g in range(G)]
-        before = low - jnp.concatenate(x, axis=0)
+        ends = box_ends(n, size, get, sums)
         for w in range(filters):
-            shift = widths[w] - 1
-            upto = pltpu.roll(jnp.where(lane < shift, high, low), LANES - shift, 1)
-            y = (upto - before) * scale[w]
+            y = box(ends, widths[w], scale[w], lane)
             for g in range(G):
                 shape = (out.shape[1], out.shape[2] // G, LANES)
                 rows_out = slice(g * shape[1], (g + 1) * shape[1])
                 out[w, :, rows_out, n * LANES : (n + 1) * LANES] = y[g * rows : (g + 1) * rows].reshape(shape)
+
+
+def late_kernel(p, filters, widths, x, filtered, out, made, matrix, lhs, sums, sems):
+    size = p.relays * p.per
+    halves = p.halves
+    tm = lax.axis_index("tm")
+    me = lax.axis_index("freq") * halves + tm
+    fill_matrix(matrix)
+    stride = p.per * (p.blocks + 1)
+
+    def get(n):
+        pieces = []
+        for k in range(p.relays):
+            if n < p.blocks:
+                v = x[pl.ds(k * stride + n, p.per, stride=p.blocks), :]
+            else:
+                v = jnp.where(tm == halves - 1, 0.0, x[pl.ds(k * stride + p.per * p.blocks, p.per), :])
+            pieces.append(v)
+        return jnp.concatenate(pieces, axis=0)
+
+    prefix_sums(p.blocks, size, get, matrix, lhs, sums)
+    lane = lax.broadcasted_iota(jnp.int32, (size, LANES), 1)
+    copies = []
+    for w in range(filters):
+        scale = box_scale(widths[w], p.all_rows, (size, LANES))
+        for n in range(p.blocks):
+            y = box(box_ends(n, size, get, sums), widths[w], scale, lane)
+            for k in range(p.relays):
+                made[w, k, :, n * LANES : (n + 1) * LANES] = y[k * p.per : (k + 1) * p.per]
+        for k in range(p.relays):
+            part = flipped(me, p.far + k, p.parts)
+            at = out.at[w, part, pl.ds((p.groups - 1) * p.per, p.per)]
+            c = pltpu.make_async_copy(made.at[w, k], at, sems.at[w, k])
+            c.start()
+            copies.append(c)
+    for c in copies:
+        c.wait()
+
+
+def filter_late(p, x, filtered, widths):
+    filters = widths.shape[0]
+    size = p.relays * p.per
+    total = size * (p.blocks + 1)
+    cells = filters * size * p.span
+    return pl.pallas_call(
+        functools.partial(late_kernel, p, filters),
+        out_shape=jax.ShapeDtypeStruct(filtered.shape, jnp.float32),
+        in_specs=[
+            pl.BlockSpec(memory_space=SMEM),
+            pl.BlockSpec(memory_space=VMEM),
+            pl.BlockSpec(memory_space=pl.ANY),
+        ],
+        out_specs=pl.BlockSpec(memory_space=pl.ANY),
+        scratch_shapes=[
+            pltpu.VMEM((filters, p.relays, p.per, p.span), jnp.float32),
+            pltpu.VMEM((2 * LANES, 2 * LANES), jnp.bfloat16),
+            pltpu.VMEM((total, 2 * LANES), jnp.bfloat16),
+            pltpu.VMEM((total, 2 * LANES), jnp.float32),
+            pltpu.SemaphoreType.DMA((filters, p.relays)),
+        ],
+        input_output_aliases={2: 0},
+        compiler_params=pltpu.CompilerParams(vmem_limit_bytes=32 << 20),
+        cost_estimate=pl.CostEstimate(flops=96 * cells, bytes_accessed=4 * cells, transcendentals=0),
+    )(widths, x, filtered)
 
 
 def filter_rows(p, xs, edges, widths):
@@ -466,6 +586,7 @@
 
 
 PARTS = 4
+RELAYS = 4
 GROUPS = 2
 
 
@@ -473,7 +594,13 @@
     rows, span = spectra.shape
     p = Plan(rows, span, *delays.shape, lax.axis_size("freq"), lax.axis_size("tm"), GROUPS)
     made = [x.reshape(-1, LANES) for x in dedisperse(p, delays, spectra)]
-    out = filter_rows(p, made[: p.groups], made[p.groups :], widths)
+    xs, edges, relay = made[: p.groups], made[p.groups : 2 * p.groups], made[2 * p.groups :]
+    if relay:
+        swap = [(f, (f + p.bands // 2) % p.bands) for f in range(p.bands)]
+        late = lax.ppermute(relay[0], "freq", swap)
+    out = filter_rows(p, xs, edges, widths)
+    if relay:
+        out = filter_late(p, late, out, widths)
     return out.reshape(widths.shape[0], rows, span)
 
 

time: 141 us -> 133 us (0.943)
  Pallas kernels: 141 us -> 123 us
  starting transfers between devices: 0 us -> 6.91 us
  waiting for transfers between devices: 0 us -> 2.92 us
    pallas_call x1, Pallas kernels: 130 us -> 109 us  [dedisperse(): pl.pallas_call(functools.partial(tree_kernel, p), out_shape=[out_shape] *...]
    ppermute x0 -> x1, starting transfers between devices: none -> 6.91 us  [local(): late = lax.ppermute(relay[0], 'freq', swap)]
    ppermute x0 -> x1, waiting for transfers between devices: none -> 2.92 us  [local(): late = lax.ppermute(relay[0], 'freq', swap)]
    pallas_call x0 -> x1, Pallas kernels: none -> 2.81 us  [filter_late(): pl.pallas_call(functools.partial(late_kernel, p, filters), out_shape=jax....]
  transfers between devices with their start and end apart: 0 -> 1, of which waited for: 0 -> 1; matrix products, arithmetic and copies ran while one was open for 0% -> 0% of each run, Pallas kernels for 0% -> 8%
where the time goes in v4:
time: 133 us
  Pallas kernels  123 us (92%)
  starting transfers between devices  6.91 us (5%)
  waiting for transfers between devices  2.92 us (2%)
    pallas_call x1, Pallas kernels, dedisperse(): pl.pallas_call(functools.partial(tree_kernel, p), out_shape=[out_shape] *...  109 us
    pallas_call x1, Pallas kernels, filter_rows(): pl.pallas_call(functools.partial(filter_kernel, p, filters, parts), grid=...  11.1 us
    ppermute x1, starting transfers between devices, local(): late = lax.ppermute(relay[0], 'freq', swap)  6.91 us
    ppermute x1, waiting for transfers between devices, local(): late = lax.ppermute(relay[0], 'freq', swap)  2.92 us
    pallas_call x1, Pallas kernels, filter_late(): pl.pallas_call(functools.partial(late_kernel, p, filters), out_shape=jax....  2.81 us
  transfers between devices with their start and end apart: 1, of which 1 were waited for; matrix products, arithmetic and copies ran while one was open for 0% of the time, Pallas kernels for 8%

profile of v4, /device:TPU:0, one launch (start us, length us, event | category | flops | bytes accessed | tf_op | source)
XLA Modules:
  0.0 133.0 jit_solution(14480612613489929993)
XLA Ops:
  0.0 109.2 %shard_map.37 = (f32[16,160,128]{2,1,0:T(8,128)}, f32[16,160,128]{2,1,0:T(8,128)}, f32[16,8,128]{2,1,0:T(8,128)}, f32[16,8,128]{2,1,0:T(8,128)}, f32[4,168,128]{2,1,0:T(8,128)}) custom-call(s32[11,2048]{1,0:T(8,128)} %delays.1, f32[256,2560]{1,0:T(8,128)} %spectra.1), custom_call_target="tpu_custom_call" | custom-call | tf_op jit(solution)/shard_map/pallas_call | solution.py:394
  109.2 6.9 %collective-permute-start = (f32[672,128]{1,0:T(8,128)}, f32[672,128]{1,0:T(8,128)S(1)}, u32[]{:S(2)}, u32[]{:S(2)}) collective-permute-start(f32[672,128]{1,0:T(8,128)} %bitcast.10), channel_id=1, source_target_pairs={{0,8},{2,10},{4,12},{6,14},{8,0},{10,2},{12,4},{14,6},{1,9},{3,11}... | collective-permute-start | bytes 1032200 | tf_op jit(solution)/shard_map/ppermute | solution.py:600
  116.1 0.0 copy-start
  116.1 11.1 %shard_map.38.filtered = f32[8,16,16,2560]{3,2,1,0:T(8,128)} custom-call(s32[8]{0:T(128)} %widths.3, f32[2560,128]{1,0:T(8,128)} %bitcast.6, f32[2560,128]{1,0:T(8,128)} %bitcast.7, f32[128,128]{1,0:T(8,128)} %bitcast.8, f32[128,128]{1,0:T(8,128)} %bitcast.9), custom_call_target="tpu_custom_call" | custom-call | flops 503316480 | bytes 20971520 | tf_op jit(solution)/shard_map/pallas_call | solution.py:570
  127.2 2.9 %collective-permute-done.x = f32[672,128]{1,0:T(8,128)S(1)} collective-permute-done((f32[672,128]{1,0:T(8,128)}, f32[672,128]{1,0:T(8,128)S(1)}, u32[]{:S(2)}, u32[]{:S(2)}) %collective-permute-start) | collective-permute-done | bytes 344096 | tf_op jit(solution)/shard_map/ppermute | solution.py:600
  130.1 0.0 copy-done
  130.1 2.8 %shard_map.39 = f32[8,16,16,2560]{3,2,1,0:T(8,128)} custom-call(s32[8]{0:T(128)S(1)} %copy-done, f32[672,128]{1,0:T(8,128)S(1)} %collective-permute-done.x, f32[8,16,16,2560]{3,2,1,0:T(8,128)} %shard_map.38.filtered), custom_call_target="tpu_custom_call", output_to_operand_aliasing={{}: (2, {})} | custom-call | flops 62914560 | bytes 2621440 | tf_op jit(solution)/shard_map/pallas_call | solution.py:536
Async XLA Ops:
  109.2 20.9 %collective-permute-start = (f32[672,128]{1,0:T(8,128)}, f32[672,128]{1,0:T(8,128)S(1)}, u32[]{:S(2)}, u32[]{:S(2)}) collective-permute-start(f32[672,128]{1,0:T(8,128)} %bitcast.10), channel_id=1, source_target_pairs={{0,8},{2,10},{4,12},{6,14},{8,0},{10,2},{12,4},{14,6},{1,9},{3,11}... | collective-permute-start | bytes 1032200 | tf_op jit(solution)/shard_map/ppermute | solution.py:600
  116.1 14.0 %copy-start = (s32[8]{0:T(128)S(1)}, s32[8]{0:T(128)}, u32[]{:S(2)}) copy-start(s32[8]{0:T(128)} %widths.3) | copy-start | bytes 100

commit v5 on v4

--- a/solution.py
+++ b/solution.py
@@ -82,9 +82,9 @@
     relay = take(1)[0] if p.relays else None
     (rows_in, lead) = take(2)
     tree_a, tree_b = take(2), take(2)
-    (send_a,) = take(1)
+    send_a = take(G)
     send_b = take(G)
-    (came_a,) = take(1)
+    came_a = take(G)
     came_b = take(G)
     ready, ready_edge = take(G), take(G)
     buf_a, buf_b = take(2)
@@ -138,7 +138,7 @@
 
         lax.fori_loop(0, p.rows // SUB, body, 0)
 
-    def several(src, pitch, first, depth, base, put):
+    def several(src, pitch, first, depth, base, put, only=None):
         lane = lax.broadcasted_iota(jnp.int32, (pitch, LANES), 1)
         half = 2**first
         rows = [src[pl.ds(pl.multiple_of((base + m * half) * pitch, SUB), pitch), :] for m in range(2**depth)]
@@ -150,14 +150,17 @@
                 a, low = rows[m], rows[m + step]
                 high = pltpu.roll(low, pitch - 1, 0)
                 for q in (m, m + step):
+                    if only is not None and q % 2 != only:
+                        continue
                     shift = own_delays[first + t, own_at + base + q * half]
                     rows[q] = a + pltpu.roll(jnp.where(lane < shift, high, low), LANES - shift, 1)
         for m, v in enumerate(rows):
-            put(base + m * half, v)
-
-    def levels(bufs, pitch, together):
+            if only is None or m % 2 == only:
+                put(base + m * half, v)
+
+    def levels(bufs, pitch, together, passes, only=None):
         src, dst = bufs
-        for first, depth in p.passes[:-1]:
+        for first, depth in passes:
             count = p.rows >> depth
             unroll = min(together, count)
 
@@ -168,7 +171,7 @@
                 for u in range(unroll):
                     q = n * unroll + u
                     base = ((q >> first) << (first + depth)) + (q & (2**first - 1))
-                    several(src, pitch, first, depth, base, put)
+                    several(src, pitch, first, depth, base, put, only)
                 return carry
 
             lax.fori_loop(0, count // unroll, body, 0)
@@ -235,7 +238,7 @@
                 c.start()
 
             copies.append((other, c))
-        c = pltpu.make_async_copy(src.at[me], dst.at[me], own_sems.at[1 + 2 * G + turn])
+        c = pltpu.make_async_copy(src.at[me], dst.at[me], own_sems.at[3 * G + turn])
 
         @pl.when(tm < halves - 1)
         def _(c=c):
@@ -272,10 +275,18 @@
     load_a.wait()
     spread(tree_a[0], p.pitch_a, 0, SUB, 0)
     load_own.wait()
-    src = levels(tree_a, p.pitch_a, 8)
-    last_levels(src, p.pitch_a, send_a, p.blocks_a, 0, p.own, 8)
-
-    pl.semaphore_wait(barrier, parts - 1)
+    sent_a = []
+    split = p.passes[1][0] if len(p.passes) > 2 and G == 2 and p.per == 2 ** p.passes[1][0] else None
+    src = levels(tree_a, p.pitch_a, 8, p.passes[:-1] if split is None else p.passes[:1])
+    for g in range(G):
+        ready_rows = src
+        if split is not None:
+            ready_rows = levels(tree_a[::-1], p.pitch_a, 8, p.passes[1:-1], g)
+        last_levels(ready_rows, p.pitch_a, send_a[g], p.blocks_a, g, p.per, 8)
+        if g == 0:
+            pl.semaphore_wait(barrier, parts - 1)
+        sent_a.append(send(send_a[g], came_a[g], g))
+
     left = (tm + halves - 1) % halves
     get_lead = pltpu.make_async_remote_copy(
         src_ref=spectra.at[:, : p.lead_blocks * LANES],
@@ -286,16 +297,15 @@
         device_id_type=MESH,
     )
     get_lead.start()
-    sent_a = send(send_a, came_a, 0)
 
     load_b.wait()
     get_lead.wait()
     spread(tree_b[0], p.pitch_b, p.blocks_a, p.blocks_b, p.lead_blocks)
-    src = levels(tree_b, p.pitch_b, 4)
+    src = levels(tree_b, p.pitch_b, 4, p.passes[:-1])
     sent_b = []
     for g in range(G):
         last_levels(src, p.pitch_b, send_b[g], p.blocks_b, g, p.per, 4)
-        sent_b.append(send(send_b[g], came_b[g], 1 + g))
+        sent_b.append(send(send_b[g], came_b[g], G + g))
 
     total, pitch, rows = p.total, p.pitch_x, p.per
     lane = lax.broadcasted_iota(jnp.int32, (total, LANES), 1)
@@ -313,15 +323,15 @@
     back, back_edges = [], []
     for c in load_bands:
         c.wait()
-    arrive(sent_a)
     for g in range(G):
+        arrive(sent_a[g])
         arrive(sent_b[g])
 
         def gather(i, carry, g=g):
             for s in range(bands):
                 at = (s * rows + i) * pitch
                 for c in range(halves):
-                    piece = came_a[s * halves + c, pl.ds((g * rows + i) * p.blocks_a, p.blocks_a), :]
+                    piece = came_a[g][s * halves + c, pl.ds(i * p.blocks_a, p.blocks_a), :]
                     buf_a[pl.ds(at + c * p.blocks, p.blocks_a), :] = piece
                     piece = came_b[g][s * halves + c, pl.ds(i * p.blocks_b, p.blocks_b), :]
                     buf_a[pl.ds(at + c * p.blocks + p.blocks_a, p.blocks_b), :] = piece
@@ -356,7 +366,7 @@
             lax.fori_loop(0, rows, one_row, 0)
             src, dst = dst, src
         left_out = range(p.far, p.far + p.relays) if g == G - 1 else ()
-        back.append(send(ready[g], outs[g], 1 + G + g, left_out))
+        back.append(send(ready[g], outs[g], 2 * G + g, left_out))
         back_edges.append(send_edges(ready_edge[g], edges[g], g, left_out))
     relayed = send_relays(ready[G - 1], ready_edge[G - 1])
     for sent, (copies, c) in zip(back, back_edges):
@@ -370,7 +380,7 @@
 
     for c in relayed:
         c.wait()
-    for sent in [sent_a] + sent_b + back:
+    for sent in sent_a + sent_b + back:
         for c in sent[0]:
             c.wait_send()
     for copies, _ in back_edges:
@@ -390,7 +400,7 @@
         relay_shapes = [jax.ShapeDtypeStruct((p.relays, p.per * (p.blocks + 1), LANES), jnp.float32)]
     here = pl.BlockSpec(memory_space=pl.ANY)
     f32 = jnp.float32
-    turns = 1 + 2 * G
+    turns = 3 * G
     return pl.pallas_call(
         functools.partial(tree_kernel, p),
         out_shape=[out_shape] * G + [edge_shape] * G + relay_shapes,
@@ -402,9 +412,9 @@
         ]
         + [pltpu.VMEM((p.rows * p.pitch_a + SUB, LANES), f32)] * 2
         + [pltpu.VMEM((p.rows * p.pitch_b + SUB, LANES), f32)] * 2
-        + [pltpu.VMEM((parts, p.own * p.blocks_a, LANES), f32)]
+        + [pltpu.VMEM((parts, p.per * p.blocks_a, LANES), f32)] * G
         + [pltpu.VMEM((parts, p.per * p.blocks_b, LANES), f32)] * G
-        + [pltpu.VMEM((parts, p.own * p.blocks_a, LANES), f32)]
+        + [pltpu.VMEM((parts, p.per * p.blocks_a, LANES), f32)] * G
         + [pltpu.VMEM((parts, p.per * p.blocks_b, LANES), f32)] * G
         + [pltpu.VMEM((parts, p.per * p.blocks, LANES), f32)] * G
         + [pltpu.VMEM((parts, p.per, LANES), f32)] * G

time: 133 us -> 132 us (level)
  Pallas kernels: 123 us -> 121 us
    pallas_call x1, Pallas kernels: 109 us -> 108 us  [dedisperse(): pl.pallas_call(functools.partial(tree_kernel, p), out_shape=[out_shape] *...]
where the time goes in v5:
time: 132 us; the launch traced here: 131 us
  Pallas kernels  121 us (92%)
  starting transfers between devices  6.99 us (5%)
  waiting for transfers between devices  3 us (2%)
    pallas_call x1, Pallas kernels, dedisperse(): pl.pallas_call(functools.partial(tree_kernel, p), out_shape=[out_shape] *...  108 us
    pallas_call x1, Pallas kernels, filter_rows(): pl.pallas_call(functools.partial(filter_kernel, p, filters, parts), grid=...  11.1 us
    ppermute x1, starting transfers between devices, local(): late = lax.ppermute(relay[0], 'freq', swap)  6.99 us
    ppermute x1, waiting for transfers between devices, local(): late = lax.ppermute(relay[0], 'freq', swap)  3 us
    pallas_call x1, Pallas kernels, filter_late(): pl.pallas_call(functools.partial(late_kernel, p, filters), out_shape=jax....  2.81 us
  transfers between devices with their start and end apart: 1, of which 1 were waited for; matrix products, arithmetic and copies ran while one was open for 0% of the time, Pallas kernels for 8%

profile of v5, /device:TPU:0, one launch (start us, length us, event | category | flops | bytes accessed | tf_op | source)
XLA Modules:
  0.0 131.4 jit_solution(12126520042170960489)
XLA Ops:
  0.0 107.5 %shard_map.37 = (f32[16,160,128]{2,1,0:T(8,128)}, f32[16,160,128]{2,1,0:T(8,128)}, f32[16,8,128]{2,1,0:T(8,128)}, f32[16,8,128]{2,1,0:T(8,128)}, f32[4,168,128]{2,1,0:T(8,128)}) custom-call(s32[11,2048]{1,0:T(8,128)} %delays.1, f32[256,2560]{1,0:T(8,128)} %spectra.1), custom_call_target="tpu_custom_call" | custom-call | tf_op jit(solution)/shard_map/pallas_call | solution.py:404
  107.5 7.0 %collective-permute-start = (f32[672,128]{1,0:T(8,128)}, f32[672,128]{1,0:T(8,128)S(1)}, u32[]{:S(2)}, u32[]{:S(2)}) collective-permute-start(f32[672,128]{1,0:T(8,128)} %bitcast.10), channel_id=1, source_target_pairs={{0,8},{2,10},{4,12},{6,14},{8,0},{10,2},{12,4},{14,6},{1,9},{3,11}... | collective-permute-start | bytes 1032200 | tf_op jit(solution)/shard_map/ppermute | solution.py:610
  114.5 0.0 copy-start
  114.5 11.1 %shard_map.38.filtered = f32[8,16,16,2560]{3,2,1,0:T(8,128)} custom-call(s32[8]{0:T(128)} %widths.3, f32[2560,128]{1,0:T(8,128)} %bitcast.6, f32[2560,128]{1,0:T(8,128)} %bitcast.7, f32[128,128]{1,0:T(8,128)} %bitcast.8, f32[128,128]{1,0:T(8,128)} %bitcast.9), custom_call_target="tpu_custom_call" | custom-call | flops 503316480 | bytes 20971520 | tf_op jit(solution)/shard_map/pallas_call | solution.py:580
  125.6 3.0 %collective-permute-done.x = f32[672,128]{1,0:T(8,128)S(1)} collective-permute-done((f32[672,128]{1,0:T(8,128)}, f32[672,128]{1,0:T(8,128)S(1)}, u32[]{:S(2)}, u32[]{:S(2)}) %collective-permute-start) | collective-permute-done | bytes 344096 | tf_op jit(solution)/shard_map/ppermute | solution.py:610
  128.6 0.0 copy-done
  128.6 2.8 %shard_map.39 = f32[8,16,16,2560]{3,2,1,0:T(8,128)} custom-call(s32[8]{0:T(128)S(1)} %copy-done, f32[672,128]{1,0:T(8,128)S(1)} %collective-permute-done.x, f32[8,16,16,2560]{3,2,1,0:T(8,128)} %shard_map.38.filtered), custom_call_target="tpu_custom_call", output_to_operand_aliasing={{}: (2, {})} | custom-call | flops 62914560 | bytes 2621440 | tf_op jit(solution)/shard_map/pallas_call | solution.py:546
Async XLA Ops:
  107.5 21.1 %collective-permute-start = (f32[672,128]{1,0:T(8,128)}, f32[672,128]{1,0:T(8,128)S(1)}, u32[]{:S(2)}, u32[]{:S(2)}) collective-permute-start(f32[672,128]{1,0:T(8,128)} %bitcast.10), channel_id=1, source_target_pairs={{0,8},{2,10},{4,12},{6,14},{8,0},{10,2},{12,4},{14,6},{1,9},{3,11}... | collective-permute-start | bytes 1032200 | tf_op jit(solution)/shard_map/ppermute | solution.py:610
  114.5 14.1 %copy-start = (s32[8]{0:T(128)S(1)}, s32[8]{0:T(128)}, u32[]{:S(2)}) copy-start(s32[8]{0:T(128)} %widths.3) | copy-start | bytes 100

commit v6 on v5

--- a/solution.py
+++ b/solution.py
@@ -60,7 +60,8 @@
         self.total = self.blocks * halves
         reach = 2 ** (all_levels - 1)
         self.pitch_x = round_up(self.total + cdiv(reach, LANES) + 2, SUB)
-        self.relays = RELAYS if self.groups > 1 and self.parts >= 2 * RELAYS else 0
+        self.late = LATE if self.groups > 1 and self.parts >= 16 else ()
+        self.relays = [k for ks in self.late for k in ks]
         self.far = self.parts // 2
         starts = list(range(0, self.levels, 3))
         self.passes = [(first, min(3, self.levels - first)) for first in starts]
@@ -79,7 +80,7 @@
         return got
 
     outs, edges = take(G), take(G)
-    relay = take(1)[0] if p.relays else None
+    relay = take(len(p.late))
     (rows_in, lead) = take(2)
     tree_a, tree_b = take(2), take(2)
     send_a = take(G)
@@ -110,8 +111,8 @@
                 delays.at[:, pl.ds(pl.multiple_of(at, LANES), LANES)], band_delays.at[j], band_sems.at[j]
             )
         )
+    load_own.start()
     load_a.start()
-    load_own.start()
     load_b.start()
     for c in load_bands:
         c.start()
@@ -126,17 +127,19 @@
 
     def spread(buf, pitch, first, count, lead_count):
         def body(n, carry):
-            at = pl.ds(pl.multiple_of(n * SUB, SUB), SUB)
-            for b in range(count):
-                v = rows_in[at, (first + b) * LANES : (first + b + 1) * LANES]
-                buf[pl.ds(n * (SUB * pitch) + b, SUB, stride=pitch), :] = v
-            for b in range(lead_count):
-                v = lead[at, b * LANES : (b + 1) * LANES]
-                v = jnp.where(tm < halves - 1, v, 0.0)
-                buf[pl.ds(n * (SUB * pitch) + count + b, SUB, stride=pitch), :] = v
+            for u in range(4):
+                q = n * 4 + u
+                at = pl.ds(pl.multiple_of(q * SUB, SUB), SUB)
+                for b in range(count):
+                    v = rows_in[at, (first + b) * LANES : (first + b + 1) * LANES]
+                    buf[pl.ds(q * (SUB * pitch) + b, SUB, stride=pitch), :] = v
+                for b in range(lead_count):
+                    v = lead[at, b * LANES : (b + 1) * LANES]
+                    v = jnp.where(tm < halves - 1, v, 0.0)
+                    buf[pl.ds(q * (SUB * pitch) + count + b, SUB, stride=pitch), :] = v
             return carry
 
-        lax.fori_loop(0, p.rows // SUB, body, 0)
+        lax.fori_loop(0, p.rows // SUB // 4, body, 0)
 
     def several(src, pitch, first, depth, base, put, only=None):
         lane = lax.broadcasted_iota(jnp.int32, (pitch, LANES), 1)
@@ -248,18 +251,19 @@
 
     def send_relays(src, src_edge):
         copies = []
-        for k in range(p.relays):
+        places = [x.at[n] for x, ks in zip(relay, p.late) for n in range(len(ks))]
+        for slot, k in enumerate(p.relays):
             other, _ = peer(p.far + k)
             for n, (x, first, size) in enumerate(((src, 0, p.per * p.blocks), (src_edge, p.per * p.blocks, p.per))):
-                to = relay.at[k, pl.ds(first, size)]
+                to = places[slot].at[pl.ds(first, size)]
                 if k == 0:
-                    c = pltpu.make_async_copy(x.at[other], to, relay_sems.at[0, n, k])
+                    c = pltpu.make_async_copy(x.at[other], to, relay_sems.at[0, n, slot])
                 else:
                     c = pltpu.make_async_remote_copy(
                         src_ref=x.at[other],
                         dst_ref=to,
-                        send_sem=relay_sems.at[0, n, k],
-                        recv_sem=relay_sems.at[1, n, k],
+                        send_sem=relay_sems.at[0, n, slot],
+                        recv_sem=relay_sems.at[1, n, slot],
                         device_id=peer(k)[1],
                         device_id_type=MESH,
                     )
@@ -365,7 +369,7 @@
 
             lax.fori_loop(0, rows, one_row, 0)
             src, dst = dst, src
-        left_out = range(p.far, p.far + p.relays) if g == G - 1 else ()
+        left_out = [p.far + k for k in p.relays] if g == G - 1 else ()
         back.append(send(ready[g], outs[g], 2 * G + g, left_out))
         back_edges.append(send_edges(ready_edge[g], edges[g], g, left_out))
     relayed = send_relays(ready[G - 1], ready_edge[G - 1])
@@ -395,9 +399,9 @@
     G, parts = p.groups, p.parts
     out_shape = jax.ShapeDtypeStruct((parts, p.per * p.blocks, LANES), jnp.float32)
     edge_shape = jax.ShapeDtypeStruct((parts, p.per, LANES), jnp.float32)
-    relay_shapes = []
-    if p.relays:
-        relay_shapes = [jax.ShapeDtypeStruct((p.relays, p.per * (p.blocks + 1), LANES), jnp.float32)]
+    relay_shapes = [
+        jax.ShapeDtypeStruct((len(ks), p.per * (p.blocks + 1), LANES), jnp.float32) for ks in p.late
+    ]
     here = pl.BlockSpec(memory_space=pl.ANY)
     f32 = jnp.float32
     turns = 3 * G
@@ -428,7 +432,7 @@
             pltpu.SemaphoreType.DMA((3,)),
             pltpu.SemaphoreType.DMA((2,)),
             pltpu.SemaphoreType.DMA((p.bands,)),
-            pltpu.SemaphoreType.DMA((2, 2, max(p.relays, 1))),
+            pltpu.SemaphoreType.DMA((2, 2, max(len(p.relays), 1))),
         ],
         compiler_params=pltpu.CompilerParams(
             collective_id=0, has_side_effects=True, vmem_limit_bytes=58 << 20
@@ -452,7 +456,8 @@
         t = (v - h.astype(jnp.float32)).astype(jnp.bfloat16)
         lhs[n * size : (n + 1) * size, :LANES] = h
         lhs[n * size : (n + 1) * size, LANES:] = t
-    sums[...] = jnp.dot(lhs[...], matrix[...], preferred_element_type=jnp.float32)
+    used = slice(0, (blocks + 1) * size)
+    sums[used, :] = jnp.dot(lhs[used, :], matrix[...], preferred_element_type=jnp.float32)
 
 
 def box_ends(n, size, get, sums):
@@ -476,33 +481,53 @@
     G = p.groups
     xs, edges, (out, matrix, lhs, sums) = refs[:G], refs[G : 2 * G], refs[2 * G :]
     rows = parts * p.per
-    size = G * rows
-    last = lax.axis_index("tm") == p.halves - 1
-
-    @pl.when(pl.program_id(0) == 0)
+    tm = lax.axis_index("tm")
+    me = lax.axis_index("freq") * p.halves + tm
+    step = pl.program_id(0)
+
+    @pl.when(step == 0)
     def _():
         fill_matrix(matrix)
 
-    def get(n):
-        if n < p.blocks:
-            return jnp.concatenate([x[pl.ds(n, rows, stride=p.blocks), :] for x in xs], axis=0)
-        return jnp.where(last, 0.0, jnp.concatenate([e[...] for e in edges], axis=0))
-
-    prefix_sums(p.blocks, size, get, matrix, lhs, sums)
-    lane = lax.broadcasted_iota(jnp.int32, (size, LANES), 1)
-    scale = [box_scale(widths[w], p.all_rows, (size, LANES)) for w in range(filters)]
-    for n in range(p.blocks):
-        ends = box_ends(n, size, get, sums)
-        for w in range(filters):
-            y = box(ends, widths[w], scale[w], lane)
-            for g in range(G):
-                shape = (out.shape[1], out.shape[2] // G, LANES)
-                rows_out = slice(g * shape[1], (g + 1) * shape[1])
-                out[w, :, rows_out, n * LANES : (n + 1) * LANES] = y[g * rows : (g + 1) * rows].reshape(shape)
-
-
-def late_kernel(p, filters, widths, x, filtered, out, made, matrix, lhs, sums, sems):
-    size = p.relays * p.per
+    def run(groups):
+        size = groups * rows
+
+        def get(n):
+            if n < p.blocks:
+                pieces = [x[pl.ds(n, rows, stride=p.blocks), :] for x in xs[:groups]]
+                return jnp.concatenate(pieces, axis=0)
+            pieces = [e[...] for e in edges[:groups]]
+            return jnp.where(tm == p.halves - 1, 0.0, jnp.concatenate(pieces, axis=0))
+
+        prefix_sums(p.blocks, size, get, matrix, lhs, sums)
+        lane = lax.broadcasted_iota(jnp.int32, (size, LANES), 1)
+        scale = [box_scale(widths[w], p.all_rows, (size, LANES)) for w in range(filters)]
+        for n in range(p.blocks):
+            ends = box_ends(n, size, get, sums)
+            for w in range(filters):
+                y = box(ends, widths[w], scale[w], lane)
+                for g in range(groups):
+                    shape = (out.shape[1], out.shape[2] // G, LANES)
+                    rows_out = slice(g * shape[1], (g + 1) * shape[1])
+                    piece = y[g * rows : (g + 1) * rows].reshape(shape)
+                    out[w, :, rows_out, n * LANES : (n + 1) * LANES] = piece
+
+    if sorted(p.relays) != list(range(parts)):
+        run(G)
+        return
+    late_step = flipped(me, p.far, p.parts) // parts
+
+    @pl.when(step != late_step)
+    def _():
+        run(G)
+
+    @pl.when(step == late_step)
+    def _():
+        run(G - 1)
+
+
+def late_kernel(p, ks, filters, widths, x, filtered, out, made, matrix, lhs, sums, sems):
+    size = len(ks) * p.per
     halves = p.halves
     tm = lax.axis_index("tm")
     me = lax.axis_index("freq") * halves + tm
@@ -511,7 +536,7 @@
 
     def get(n):
         pieces = []
-        for k in range(p.relays):
+        for k in range(len(ks)):
             if n < p.blocks:
                 v = x[pl.ds(k * stride + n, p.per, stride=p.blocks), :]
             else:
@@ -526,25 +551,25 @@
         scale = box_scale(widths[w], p.all_rows, (size, LANES))
         for n in range(p.blocks):
             y = box(box_ends(n, size, get, sums), widths[w], scale, lane)
-            for k in range(p.relays):
+            for k in range(len(ks)):
                 made[w, k, :, n * LANES : (n + 1) * LANES] = y[k * p.per : (k + 1) * p.per]
-        for k in range(p.relays):
+        for slot, k in enumerate(ks):
             part = flipped(me, p.far + k, p.parts)
             at = out.at[w, part, pl.ds((p.groups - 1) * p.per, p.per)]
-            c = pltpu.make_async_copy(made.at[w, k], at, sems.at[w, k])
+            c = pltpu.make_async_copy(made.at[w, slot], at, sems.at[w, slot])
             c.start()
             copies.append(c)
     for c in copies:
         c.wait()
 
 
-def filter_late(p, x, filtered, widths):
+def filter_late(p, ks, x, filtered, widths):
     filters = widths.shape[0]
-    size = p.relays * p.per
+    size = len(ks) * p.per
     total = size * (p.blocks + 1)
     cells = filters * size * p.span
     return pl.pallas_call(
-        functools.partial(late_kernel, p, filters),
+        functools.partial(late_kernel, p, ks, filters),
         out_shape=jax.ShapeDtypeStruct(filtered.shape, jnp.float32),
         in_specs=[
             pl.BlockSpec(memory_space=SMEM),
@@ -553,11 +578,11 @@
         ],
         out_specs=pl.BlockSpec(memory_space=pl.ANY),
         scratch_shapes=[
-            pltpu.VMEM((filters, p.relays, p.per, p.span), jnp.float32),
+            pltpu.VMEM((filters, len(ks), p.per, p.span), jnp.float32),
             pltpu.VMEM((2 * LANES, 2 * LANES), jnp.bfloat16),
             pltpu.VMEM((total, 2 * LANES), jnp.bfloat16),
             pltpu.VMEM((total, 2 * LANES), jnp.float32),
-            pltpu.SemaphoreType.DMA((filters, p.relays)),
+            pltpu.SemaphoreType.DMA((filters, len(ks))),
         ],
         input_output_aliases={2: 0},
         compiler_params=pltpu.CompilerParams(vmem_limit_bytes=32 << 20),
@@ -596,7 +621,7 @@
 
 
 PARTS = 4
-RELAYS = 4
+LATE = ((0, 1), (2, 3))
 GROUPS = 2
 
 
@@ -605,12 +630,11 @@
     p = Plan(rows, span, *delays.shape, lax.axis_size("freq"), lax.axis_size("tm"), GROUPS)
     made = [x.reshape(-1, LANES) for x in dedisperse(p, delays, spectra)]
     xs, edges, relay = made[: p.groups], made[p.groups : 2 * p.groups], made[2 * p.groups :]
-    if relay:
-        swap = [(f, (f + p.bands // 2) % p.bands) for f in range(p.bands)]
-        late = lax.ppermute(relay[0], "freq", swap)
+    swap = [(f, (f + p.bands // 2) % p.bands) for f in range(p.bands)]
+    relay = [lax.ppermute(x, "freq", swap) for x in relay]
     out = filter_rows(p, xs, edges, widths)
-    if relay:
-        out = filter_late(p, late, out, widths)
+    for ks, x in zip(p.late, relay):
+        out = filter_late(p, ks, x, out, widths)
     return out.reshape(widths.shape[0], rows, span)
 
 

time: 132 us -> 131 us (level)
  Pallas kernels: 121 us -> 123 us
  waiting for transfers between devices: 3 us -> 1.11 us
    ppermute x1 -> x2, waiting for transfers between devices: 3 us -> 1.11 us  [local(): relay = [lax.ppermute(x, 'freq', swap) for x in relay]]
    pallas_call x1 -> x2, Pallas kernels: 2.81 us -> 4.36 us  [filter_late(): pl.pallas_call(functools.partial(late_kernel, p, ks, filters), out_shape=...]
    ppermute x1 -> x2, starting transfers between devices: 6.99 us -> 7.07 us  [local(): relay = [lax.ppermute(x, 'freq', swap) for x in relay]]
  transfers between devices with their start and end apart: 1 -> 2, of which waited for: 1 -> 1; matrix products, arithmetic and copies ran while one was open for 0% -> 0% of each run, Pallas kernels for 8% -> 10%
where the time goes in v6:
time: 131 us
  Pallas kernels  123 us (94%)
  starting transfers between devices  7.07 us (5%)
    pallas_call x1, Pallas kernels, dedisperse(): pl.pallas_call(functools.partial(tree_kernel, p), out_shape=[out_shape] *...  107 us
    pallas_call x1, Pallas kernels, filter_rows(): pl.pallas_call(functools.partial(filter_kernel, p, filters, parts), grid=...  11.2 us
    ppermute x2, starting transfers between devices, local(): relay = [lax.ppermute(x, 'freq', swap) for x in relay]  7.07 us
    pallas_call x2, Pallas kernels, filter_late(): pl.pallas_call(functools.partial(late_kernel, p, ks, filters), out_shape=...  4.36 us
  transfers between devices with their start and end apart: 2, of which 1 were waited for; matrix products, arithmetic and copies ran while one was open for 0% of the time, Pallas kernels for 10%

profile of v6, /device:TPU:0, one launch (start us, length us, event | category | flops | bytes accessed | tf_op | source)
XLA Modules:
  0.0 131.2 jit_solution(3469657932961976664)
XLA Ops:
  0.0 0.0 copy-start
  0.0 107.4 %shard_map.37 = (f32[16,160,128]{2,1,0:T(8,128)}, f32[16,160,128]{2,1,0:T(8,128)}, f32[16,8,128]{2,1,0:T(8,128)}, f32[16,8,128]{2,1,0:T(8,128)}, f32[2,168,128]{2,1,0:T(8,128)}, /*index=5*/f32[2,168,128]{2,1,0:T(8,128)}) custom-call(s32[11,2048]{1,0:T(8,128)} %delays.1, f32[256,2560]{1,0:T(8,128)} %spectra.1), custom_call_target="tpu_custom_call" | custom-call | tf_op jit(solution)/shard_map/pallas_call | solution.py:408
  107.4 7.0 %collective-permute-start.1 = (f32[336,128]{1,0:T(8,128)}, f32[336,128]{1,0:T(8,128)S(1)}, u32[]{:S(2)}, u32[]{:S(2)}) collective-permute-start(f32[336,128]{1,0:T(8,128)} %bitcast.12), channel_id=1, source_target_pairs={{0,8},{2,10},{4,12},{6,14},{8,0},{10,2},{12,4},{14,6},{1,9},{3,11}... | collective-permute-start | bytes 516104 | tf_op jit(solution)/shard_map/ppermute | solution.py:634
  114.4 0.1 collective-permute-start
  114.5 11.2 %shard_map.38.filtered = f32[8,16,16,2560]{3,2,1,0:T(8,128)} custom-call(s32[8]{0:T(128)} %widths.5, f32[2560,128]{1,0:T(8,128)} %bitcast.7, f32[2560,128]{1,0:T(8,128)} %bitcast.8, f32[128,128]{1,0:T(8,128)} %bitcast.9, f32[128,128]{1,0:T(8,128)} %bitcast.10), custom_call_target="tpu_custom_call" | custom-call | flops 503316480 | bytes 20971520 | tf_op jit(solution)/shard_map/pallas_call | solution.py:605
  125.7 1.1 collective-permute-done.1.x
  126.8 0.0 copy-done
  126.8 2.2 %shard_map.39.filtered = f32[8,16,16,2560]{3,2,1,0:T(8,128)} custom-call(s32[8]{0:T(128)S(1)} %copy-done, f32[336,128]{1,0:T(8,128)S(1)} %collective-permute-done.1.x, f32[8,16,16,2560]{3,2,1,0:T(8,128)} %shard_map.38.filtered), custom_call_target="tpu_custom_call", output_to_operand_aliasing={{}: (2, {})} | custom-call | flops 31457280 | bytes 1310720 | tf_op jit(solution)/shard_map/pallas_call | solution.py:571
  129.0 0.0 collective-permute-done.x
  129.0 2.2 %shard_map.40 = f32[8,16,16,2560]{3,2,1,0:T(8,128)} custom-call(s32[8]{0:T(128)S(1)} %copy-done, f32[336,128]{1,0:T(8,128)S(1)} %collective-permute-done.x, f32[8,16,16,2560]{3,2,1,0:T(8,128)} %shard_map.39.filtered), custom_call_target="tpu_custom_call", output_to_operand_aliasing={{}: (2, {})} | custom-call | flops 31457280 | bytes 1310720 | tf_op jit(solution)/shard_map/pallas_call | solution.py:571
Async XLA Ops:
  0.0 126.8 %copy-start = (s32[8]{0:T(128)S(1)}, s32[8]{0:T(128)}, u32[]{:S(2)}) copy-start(s32[8]{0:T(128)} %widths.5) | copy-start | bytes 100
  107.4 19.4 %collective-permute-start.1 = (f32[336,128]{1,0:T(8,128)}, f32[336,128]{1,0:T(8,128)S(1)}, u32[]{:S(2)}, u32[]{:S(2)}) collective-permute-start(f32[336,128]{1,0:T(8,128)} %bitcast.12), channel_id=1, source_target_pairs={{0,8},{2,10},{4,12},{6,14},{8,0},{10,2},{12,4},{14,6},{1,9},{3,11}... | collective-permute-start | bytes 516104 | tf_op jit(solution)/shard_map/ppermute | solution.py:634
  114.4 14.6 %collective-permute-start = (f32[336,128]{1,0:T(8,128)}, f32[336,128]{1,0:T(8,128)S(1)}, u32[]{:S(2)}, u32[]{:S(2)}) collective-permute-start(f32[336,128]{1,0:T(8,128)} %bitcast.11), channel_id=1, source_target_pairs={{0,8},{2,10},{4,12},{6,14},{8,0},{10,2},{12,4},{14,6},{1,9},{3,11}... | collective-permute-start | bytes 516104 | tf_op jit(solution)/shard_map/ppermute | solution.py:634

commit v7 on v5

--- a/solution.py
+++ b/solution.py
@@ -110,8 +110,8 @@
                 delays.at[:, pl.ds(pl.multiple_of(at, LANES), LANES)], band_delays.at[j], band_sems.at[j]
             )
         )
+    load_own.start()
     load_a.start()
-    load_own.start()
     load_b.start()
     for c in load_bands:
         c.start()
@@ -126,17 +126,19 @@
 
     def spread(buf, pitch, first, count, lead_count):
         def body(n, carry):
-            at = pl.ds(pl.multiple_of(n * SUB, SUB), SUB)
-            for b in range(count):
-                v = rows_in[at, (first + b) * LANES : (first + b + 1) * LANES]
-                buf[pl.ds(n * (SUB * pitch) + b, SUB, stride=pitch), :] = v
-            for b in range(lead_count):
-                v = lead[at, b * LANES : (b + 1) * LANES]
-                v = jnp.where(tm < halves - 1, v, 0.0)
-                buf[pl.ds(n * (SUB * pitch) + count + b, SUB, stride=pitch), :] = v
+            for u in range(4):
+                q = n * 4 + u
+                at = pl.ds(pl.multiple_of(q * SUB, SUB), SUB)
+                for b in range(count):
+                    v = rows_in[at, (first + b) * LANES : (first + b + 1) * LANES]
+                    buf[pl.ds(q * (SUB * pitch) + b, SUB, stride=pitch), :] = v
+                for b in range(lead_count):
+                    v = lead[at, b * LANES : (b + 1) * LANES]
+                    v = jnp.where(tm < halves - 1, v, 0.0)
+                    buf[pl.ds(q * (SUB * pitch) + count + b, SUB, stride=pitch), :] = v
             return carry
 
-        lax.fori_loop(0, p.rows // SUB, body, 0)
+        lax.fori_loop(0, p.rows // SUB // 4, body, 0)
 
     def several(src, pitch, first, depth, base, put, only=None):
         lane = lax.broadcasted_iota(jnp.int32, (pitch, LANES), 1)

time: 132 us -> 132 us (level)
  no operation moved by 1% of the time
where the time goes in v7:
time: 132 us; the launch traced here: 131 us
  Pallas kernels  121 us (92%)
  starting transfers between devices  6.99 us (5%)
  waiting for transfers between devices  3.07 us (2%)
    pallas_call x1, Pallas kernels, dedisperse(): pl.pallas_call(functools.partial(tree_kernel, p), out_shape=[out_shape] *...  107 us
    pallas_call x1, Pallas kernels, filter_rows(): pl.pallas_call(functools.partial(filter_kernel, p, filters, parts), grid=...  11.1 us
    ppermute x1, starting transfers between devices, local(): late = lax.ppermute(relay[0], 'freq', swap)  6.99 us
    ppermute x1, waiting for transfers between devices, local(): late = lax.ppermute(relay[0], 'freq', swap)  3.07 us
    pallas_call x1, Pallas kernels, filter_late(): pl.pallas_call(functools.partial(late_kernel, p, filters), out_shape=jax....  2.81 us
  transfers between devices with their start and end apart: 1, of which 1 were waited for; matrix products, arithmetic and copies ran while one was open for 0% of the time, Pallas kernels for 8%

profile of v7, /device:TPU:0, one launch (start us, length us, event | category | flops | bytes accessed | tf_op | source)
XLA Modules:
  0.0 131.4 jit_solution(9854602007975211463)
XLA Ops:
  0.0 107.4 %shard_map.37 = (f32[16,160,128]{2,1,0:T(8,128)}, f32[16,160,128]{2,1,0:T(8,128)}, f32[16,8,128]{2,1,0:T(8,128)}, f32[16,8,128]{2,1,0:T(8,128)}, f32[4,168,128]{2,1,0:T(8,128)}) custom-call(s32[11,2048]{1,0:T(8,128)} %delays.1, f32[256,2560]{1,0:T(8,128)} %spectra.1), custom_call_target="tpu_custom_call" | custom-call | tf_op jit(solution)/shard_map/pallas_call | solution.py:406
  107.4 7.0 %collective-permute-start = (f32[672,128]{1,0:T(8,128)}, f32[672,128]{1,0:T(8,128)S(1)}, u32[]{:S(2)}, u32[]{:S(2)}) collective-permute-start(f32[672,128]{1,0:T(8,128)} %bitcast.10), channel_id=1, source_target_pairs={{0,8},{2,10},{4,12},{6,14},{8,0},{10,2},{12,4},{14,6},{1,9},{3,11}... | collective-permute-start | bytes 1032200 | tf_op jit(solution)/shard_map/ppermute | solution.py:612
  114.4 0.0 copy-start
  114.4 11.1 %shard_map.38.filtered = f32[8,16,16,2560]{3,2,1,0:T(8,128)} custom-call(s32[8]{0:T(128)} %widths.3, f32[2560,128]{1,0:T(8,128)} %bitcast.6, f32[2560,128]{1,0:T(8,128)} %bitcast.7, f32[128,128]{1,0:T(8,128)} %bitcast.8, f32[128,128]{1,0:T(8,128)} %bitcast.9), custom_call_target="tpu_custom_call" | custom-call | flops 503316480 | bytes 20971520 | tf_op jit(solution)/shard_map/pallas_call | solution.py:582
  125.5 3.1 %collective-permute-done.x = f32[672,128]{1,0:T(8,128)S(1)} collective-permute-done((f32[672,128]{1,0:T(8,128)}, f32[672,128]{1,0:T(8,128)S(1)}, u32[]{:S(2)}, u32[]{:S(2)}) %collective-permute-start) | collective-permute-done | bytes 344096 | tf_op jit(solution)/shard_map/ppermute | solution.py:612
  128.5 0.0 copy-done
  128.5 2.8 %shard_map.39 = f32[8,16,16,2560]{3,2,1,0:T(8,128)} custom-call(s32[8]{0:T(128)S(1)} %copy-done, f32[672,128]{1,0:T(8,128)S(1)} %collective-permute-done.x, f32[8,16,16,2560]{3,2,1,0:T(8,128)} %shard_map.38.filtered), custom_call_target="tpu_custom_call", output_to_operand_aliasing={{}: (2, {})} | custom-call | flops 62914560 | bytes 2621440 | tf_op jit(solution)/shard_map/pallas_call | solution.py:548
Async XLA Ops:
  107.4 21.1 %collective-permute-start = (f32[672,128]{1,0:T(8,128)}, f32[672,128]{1,0:T(8,128)S(1)}, u32[]{:S(2)}, u32[]{:S(2)}) collective-permute-start(f32[672,128]{1,0:T(8,128)} %bitcast.10), channel_id=1, source_target_pairs={{0,8},{2,10},{4,12},{6,14},{8,0},{10,2},{12,4},{14,6},{1,9},{3,11}... | collective-permute-start | bytes 1032200 | tf_op jit(solution)/shard_map/ppermute | solution.py:612
  114.4 14.1 %copy-start = (s32[8]{0:T(128)S(1)}, s32[8]{0:T(128)}, u32[]{:S(2)}) copy-start(s32[8]{0:T(128)} %widths.3) | copy-start | bytes 100
